TPU v7x, 32 devices: a whole 2x2x4 slice. The times are simulated.
32 devices in a mesh: dp: 16 (over z, y, x), head: 2 (over core).
Axes of the slice: x: 2, y: 2, z: 4, core: 2. Of those that a mesh axis runs over, the one named last changes fastest.
Arguments:
- hidden_states: bfloat16 [32768, 768], P(('dp', 'head')), may hold values from -6 to 6
- segment_ids: int32 [32768], P(('dp', 'head')), may hold values from -1 to 1023, as said below
- input_weight: bfloat16 [768, 2304], P('dp'), may hold values from -0.21875 to 0.21875
- output_weight: bfloat16 [768, 768], P('dp'), may hold values from -0.5 to 0.5
- expand_weight: bfloat16 [768, 3072], P('dp'), may hold values from -0.21875 to 0.21875
- reduce_weight: bfloat16 [3072, 768], P('dp'), may hold values from -0.15625 to 0.15625
- adapter_down: bfloat16 [2, 768, 64], replicated, may hold values from -0.21875 to 0.21875
- adapter_down_bias: float32 [2, 64], replicated, may hold values from -3 to 3
- adapter_up: bfloat16 [2, 64, 768], replicated, may hold values from -1 to 1
- adapter_up_bias: float32 [2, 768], replicated, may hold values from -2 to 2
- norm_gain: float32 [2, 768], replicated, may hold values from 0.5 to 1.5
- norm_shift: float32 [2, 768], replicated, may hold values from -2 to 2
- output_grad: bfloat16 [32768, 768], P(('dp', 'head')), may hold values from -6 to 6
Outputs:
- layer_output: bfloat16 [32768, 768], P(('dp', 'head'))
- input_grad: float32 [32768, 768], P(('dp', 'head'))
- norm_ratio: float32 [2], replicated
- down_grad: float32 [2, 768, 64], replicated
- down_bias_grad: float32 [2, 64], replicated
- up_grad: float32 [2, 64, 768], replicated
- up_bias_grad: float32 [2, 768], replicated
- gain_grad: float32 [2, 768], replicated
- shift_grad: float32 [2, 768], replicated
Inputs may be any that keep to these rules, and one draw needn't show every extreme that they name: `segment_ids`: in each sequence of 512 positions the valid positions come first (a multiple of 32) and the rest carry -1; a valid position of sequence s carries s * 16 (512 / 32) plus the number of its item within the sequence; items hold 32 positions, or one item covers the whole sequence.
All inputs are finite; a program needn't handle non-finite values.
Results may differ from a plain program's by a relative error of at most 0.015.
Values may be sent and summed in bfloat16 or wider, within the bound.
A program may use at most 192 MiB of HBM per device.

v0:
```python
import jax
import jax.numpy as jnp
from jax import lax
from jax.experimental import pallas as pl
from jax.experimental.pallas import tpu as pltpu
from jax.sharding import PartitionSpec as P

MESH = pl.DeviceIdType.MESH
PLANE = 4


def gather_kernel(depth, *refs):
    shards, outs = refs[:4], refs[4:8]
    own_sem, send_sem, recv_sem, pair_send, pair_recv = refs[8:]
    me = lax.axis_index("dp")
    core = lax.axis_index("head")
    z = me // PLANE
    step_a = 1 + core
    step_b = 2 - core
    a = (me // step_a) % 2
    b = (me // step_b) % 2
    peer_a = z * PLANE + (1 - a) * step_a + b * step_b
    peer_b = z * PLANE + a * step_a + (1 - b) * step_b
    up, down = me + PLANE, me - PLANE
    has_up, has_down = z < depth - 1, z > 0
    partner = 1 - core

    def owner(z_of, a_of, b_of):
        return z_of * PLANE + a_of * step_a + b_of * step_b

    barrier = pltpu.get_barrier_semaphore()

    def greet(cond, target):
        def signal():
            pl.semaphore_signal(barrier, inc=1, device_id=target, device_id_type=MESH)

        if cond is None:
            signal()
        else:
            pl.when(cond)(signal)

    greet(None, {"dp": peer_a})
    greet(None, {"dp": peer_b})
    greet(None, {"head": partner})
    greet(has_up, {"dp": up})
    greet(has_down, {"dp": down})
    pl.semaphore_wait(barrier, 3 + has_up.astype(jnp.int32) + has_down.astype(jnp.int32))

    pending = []

    def guarded(cond, act):
        if cond is None:
            act()
        else:
            pl.when(cond)(act)

    def send(cond, w, piece, src, dst, direction, slot, target):
        copy = pltpu.make_async_remote_copy(
            src_ref=src,
            dst_ref=dst,
            send_sem=send_sem.at[w, direction, slot],
            recv_sem=recv_sem.at[w, piece],
            device_id=target,
            device_id_type=MESH,
        )
        guarded(cond, copy.start)
        pending.append((cond, copy))

    def hand(cond, w, piece, view):
        copy = pltpu.make_async_remote_copy(
            src_ref=view,
            dst_ref=view,
            send_sem=pair_send.at[w, piece],
            recv_sem=pair_recv.at[w, piece],
            device_id={"head": partner},
            device_id_type=MESH,
        )
        guarded(cond, copy.start)
        pending.append((cond, copy))

    def both(x, y):
        return y if x is None else (x if y is None else jnp.logical_and(x, y))

    def view_of(w, piece):
        half = outs[w].shape[2] // 2
        return outs[w].at[piece, :, pl.ds(pl.multiple_of(core * half, 128), half)]

    def arrive(cond, w, piece):
        view = view_of(w, piece)

        def wait():
            pltpu.make_async_copy(view, view, recv_sem.at[w, piece]).wait()

        guarded(cond, wait)
        return view

    def start_own(w):
        half = outs[w].shape[2] // 2
        src = shards[w].at[:, pl.ds(pl.multiple_of(core * half, 128), half)]
        view = view_of(w, me)
        send(None, w, me, src, view, 0, 0, {"dp": peer_a})
        send(has_up, w, me, src, view, 1, 0, {"dp": up})
        send(has_down, w, me, src, view, 2, 0, {"dp": down})
        send(None, w, me, src, view, 3, 0, {"dp": peer_b})
        pltpu.make_async_copy(shards[w], outs[w].at[me], own_sem.at[w]).start()

    def first(w):
        piece = peer_a
        view = arrive(None, w, piece)
        send(has_up, w, piece, view, view, 1, 1, {"dp": up})
        send(has_down, w, piece, view, view, 2, 1, {"dp": down})
        send(None, w, piece, view, view, 3, 1, {"dp": peer_b})
        hand(None, w, piece, view)

    def line(w, dist):
        for k, a_of in enumerate((a, 1 - a)):
            slot = 2 * dist + k
            below = z >= dist
            piece = owner(z - dist, a_of, b)
            view = arrive(below, w, piece)
            send(both(below, has_up), w, piece, view, view, 1, slot, {"dp": up})
            send(below, w, piece, view, view, 3, slot, {"dp": peer_b})
            hand(below, w, piece, view)
            above = z + dist < depth
            piece = owner(z + dist, a_of, b)
            view = arrive(above, w, piece)
            send(both(above, has_down), w, piece, view, view, 2, slot, {"dp": down})
            send(above, w, piece, view, view, 3, 2 * depth + slot, {"dp": peer_b})
            hand(above, w, piece, view)

    def last(w):
        for z_of in range(depth):
            for a_of in range(2):
                piece = owner(z_of, a_of, 1 - b)
                view = arrive(None, w, piece)
                hand(None, w, piece, view)

    count = len(outs)
    for w in range(count):
        start_own(w)
        first(w)
        for dist in range(1, depth):
            line(w, dist)
            if w > 0 and dist == 1:
                last(w - 1)
    last(count - 1)

    for w in range(count):
        pltpu.make_async_copy(shards[w], outs[w].at[me], own_sem.at[w]).wait()
        half = outs[w].shape[2] // 2
        for z_of in range(depth):
            for a_of in range(2):
                for b_of in range(2):
                    piece = owner(z_of, a_of, b_of)
                    other = pl.ds(pl.multiple_of((1 - core) * half, 128), half)

                    def wait_pair(w=w, piece=piece, other=other):
                        view = outs[w].at[piece, :, other]
                        pltpu.make_async_copy(view, view, pair_recv.at[w, piece]).wait()

                    pl.when(piece != me)(wait_pair)
    for cond, copy in pending:
        guarded(cond, copy.wait_send)


def gather_weights(weights):
    size = lax.axis_size("dp")
    if size % PLANE or any(w.shape[0] % 16 or w.shape[1] % 256 for w in weights):
        return [lax.all_gather(w, "dp", axis=0, tiled=True) for w in weights]
    depth = size // PLANE
    count = len(weights)
    gathered = pl.pallas_call(
        lambda *refs: gather_kernel(depth, *refs),
        out_shape=[jax.ShapeDtypeStruct((size,) + w.shape, w.dtype) for w in weights],
        in_specs=[pl.BlockSpec(memory_space=pltpu.VMEM)] * count,
        out_specs=[pl.BlockSpec(memory_space=pl.ANY)] * count,
        scratch_shapes=[
            pltpu.SemaphoreType.DMA((count,)),
            pltpu.SemaphoreType.DMA((count, 4, 4 * depth)),
            pltpu.SemaphoreType.DMA((count, size)),
            pltpu.SemaphoreType.DMA((count, size)),
            pltpu.SemaphoreType.DMA((count, size)),
        ],
        compiler_params=pltpu.CompilerParams(collective_id=0, has_side_effects=True),
        name="gather_weights",
    )(*weights)
    return [g.reshape(size * w.shape[0], w.shape[1]) for g, w in zip(gathered, weights)]


HEAD_DIM = 64
SEQ_LEN = 512
PAIR = 2 * HEAD_DIM
LOG2E = 1.4426950408889634
EPS_NORM = 1e-12
EPS_RATIO = 1e-06
SCORE_SCALE = 0.125
VMEM_LIMIT = 60 * 1024 * 1024

TAIL_POLY = (
    0.09973556672,
    0.09973643158,
    0.09346635627,
    0.08160309818,
    0.05897520771,
    0.06369893559,
    -0.03171721207,
    0.0955967654,
    -0.08087713545,
    0.01978196913,
)
INV_SQRT_2PI = 0.3989422804014327


def gelu_pair(x):
    t = 1.0 / (1.0 + 0.25 * jnp.abs(x))
    poly = jnp.full_like(t, TAIL_POLY[-1])
    for coef in TAIL_POLY[-2::-1]:
        poly = poly * t + coef
    bell = jnp.exp2(x * x * (-0.5 * LOG2E))
    below = bell * (t * poly)
    cdf = jnp.where(x >= 0, 1.0 - below, below)
    return x * cdf, cdf + x * (bell * INV_SQRT_2PI)


def dot(a, b):
    return jnp.dot(a, b, preferred_element_type=jnp.float32)


def dot_nt(a, b):
    return lax.dot_general(a, b, (((1,), (1,)), ((), ())), preferred_element_type=jnp.float32)


def dot_tn(a, b):
    return lax.dot_general(a, b, (((0,), (0,)), ((), ())), preferred_element_type=jnp.float32)


def score_bias(seg_row):
    across = jnp.broadcast_to(seg_row, (SEQ_LEN, SEQ_LEN))
    tall = jnp.broadcast_to(seg_row, (PAIR, SEQ_LEN)).T
    along = jnp.concatenate([tall] * (SEQ_LEN // PAIR), axis=1)
    row = lax.broadcasted_iota(jnp.int32, (SEQ_LEN, SEQ_LEN), 0)
    col = lax.broadcasted_iota(jnp.int32, (SEQ_LEN, SEQ_LEN), 1)
    allowed = ((across == along) & (across >= 0)) | (row == col)
    return jnp.where(allowed, 0.0, -1e30)


def head_lanes():
    lane = lax.broadcasted_iota(jnp.int32, (1, PAIR), 1)
    first = (lane < HEAD_DIM).astype(jnp.float32)
    return lane < HEAD_DIM, (first.astype(jnp.bfloat16), (1.0 - first).astype(jnp.bfloat16))


def cols(start, width):
    return pl.ds(pl.multiple_of(start, 128), width)


def attend_kernel(width, hid_ref, seg_ref, w_ref, qkv_ref, ctx_ref, bias_ref):
    step = 256

    def project(c, _):
        at = cols(c * step, step)
        qkv_ref[:, at] = dot(hid_ref[...], w_ref[:, at]).astype(jnp.bfloat16)
        return 0

    lax.fori_loop(0, 3 * width // step, project, 0)
    bias_ref[...] = score_bias(seg_ref[0])
    low, masks = head_lanes()

    def pair(h, _):
        q = qkv_ref[:, cols(h * PAIR, PAIR)]
        k = qkv_ref[:, cols(width + h * PAIR, PAIR)]
        v = qkv_ref[:, cols(2 * width + h * PAIR, PAIR)]
        v_ones = jnp.concatenate([v, jnp.ones_like(v)], axis=1)
        parts = []
        for mask in masks:
            s = dot_nt(q * mask, k) * (SCORE_SCALE * LOG2E) + bias_ref[...]
            e = jnp.exp2(s - jnp.max(s, axis=1, keepdims=True)).astype(jnp.bfloat16)
            o = dot(e, v_ones)
            parts.append(o[:, :PAIR] / o[:, PAIR:])
        ctx_ref[:, cols(h * PAIR, PAIR)] = jnp.where(low, parts[0], parts[1]).astype(jnp.bfloat16)
        return 0

    lax.fori_loop(0, width // PAIR, pair, 0)


def attend_forward(hidden, seg_rows, weight_in):
    rows, width = hidden.shape
    seqs = rows // SEQ_LEN
    return pl.pallas_call(
        lambda *refs: attend_kernel(width, *refs),
        grid=(seqs,),
        out_shape=[
            jax.ShapeDtypeStruct((rows, 3 * width), jnp.bfloat16),
            jax.ShapeDtypeStruct((rows, width), jnp.bfloat16),
        ],
        in_specs=[
            pl.BlockSpec((SEQ_LEN, width), lambda i: (i, 0)),
            pl.BlockSpec((1, 1, SEQ_LEN), lambda i: (i, 0, 0)),
            pl.BlockSpec((width, 3 * width), lambda i: (0, 0)),
        ],
        out_specs=[
            pl.BlockSpec((SEQ_LEN, 3 * width), lambda i: (i, 0)),
            pl.BlockSpec((SEQ_LEN, width), lambda i: (i, 0)),
        ],
        scratch_shapes=[pltpu.VMEM((SEQ_LEN, SEQ_LEN), jnp.float32)],
        compiler_params=pltpu.CompilerParams(vmem_limit_bytes=VMEM_LIMIT),
        cost_estimate=pl.CostEstimate(
            flops=rows * width * (6 * width + 4 * SEQ_LEN),
            bytes_accessed=2 * rows * 5 * width + 6 * width * width,
            transcendentals=rows * SEQ_LEN * width // HEAD_DIM,
        ),
        name="attend_forward",
    )(hidden, seg_rows, weight_in)


def attend_grad_kernel(width, qkv_ref, cg_ref, seg_ref, sog_ref, w_ref, out_ref, grad_ref, bias_ref):
    bias_ref[...] = score_bias(seg_ref[0])
    low, masks = head_lanes()

    def pair(h, _):
        q = qkv_ref[:, cols(h * PAIR, PAIR)]
        k = qkv_ref[:, cols(width + h * PAIR, PAIR)]
        v = qkv_ref[:, cols(2 * width + h * PAIR, PAIR)]
        g = cg_ref[:, cols(h * PAIR, PAIR)]
        parts = []
        for mask in masks:
            s = dot_nt(k * mask, q) * (SCORE_SCALE * LOG2E) + bias_ref[...]
            e = jnp.exp2(s - jnp.max(s, axis=0, keepdims=True))
            p = e * (1.0 / jnp.sum(e, axis=0, keepdims=True))
            pg = dot_nt(v * mask, g)
            ds = (p * (pg - jnp.sum(p * pg, axis=0, keepdims=True))).astype(jnp.bfloat16)
            parts.append((dot_tn(ds, k), dot(ds, q), dot(p.astype(jnp.bfloat16), g)))
        for n, scale in enumerate((SCORE_SCALE, SCORE_SCALE, 1.0)):
            both = jnp.where(low, parts[0][n], parts[1][n]) * scale
            grad_ref[:, cols(n * width + h * PAIR, PAIR)] = both.astype(jnp.bfloat16)
        return 0

    lax.fori_loop(0, width // PAIR, pair, 0)
    step = 256

    def back(c, _):
        at = cols(c * step, step)
        out_ref[:, at] = sog_ref[:, at] + dot_nt(grad_ref[...], w_ref[at, :])
        return 0

    lax.fori_loop(0, width // step, back, 0)


def attend_backward(qkv, ctx_grad, seg_rows, sum_one_grad, weight_in):
    rows, width = ctx_grad.shape
    return pl.pallas_call(
        lambda *refs: attend_grad_kernel(width, *refs),
        grid=(rows // SEQ_LEN,),
        out_shape=jax.ShapeDtypeStruct((rows, width), jnp.float32),
        in_specs=[
            pl.BlockSpec((SEQ_LEN, 3 * width), lambda i: (i, 0)),
            pl.BlockSpec((SEQ_LEN, width), lambda i: (i, 0)),
            pl.BlockSpec((1, 1, SEQ_LEN), lambda i: (i, 0, 0)),
            pl.BlockSpec((SEQ_LEN, width), lambda i: (i, 0)),
            pl.BlockSpec((width, 3 * width), lambda i: (0, 0)),
        ],
        out_specs=pl.BlockSpec((SEQ_LEN, width), lambda i: (i, 0)),
        scratch_shapes=[
            pltpu.VMEM((SEQ_LEN, 3 * width), jnp.bfloat16),
            pltpu.VMEM((SEQ_LEN, SEQ_LEN), jnp.float32),
        ],
        compiler_params=pltpu.CompilerParams(vmem_limit_bytes=VMEM_LIMIT),
        cost_estimate=pl.CostEstimate(
            flops=rows * width * (6 * width + 10 * SEQ_LEN),
            bytes_accessed=2 * rows * 8 * width + 6 * width * width,
            transcendentals=rows * SEQ_LEN * width // HEAD_DIM,
        ),
        name="attend_backward",
    )(qkv, ctx_grad, seg_rows, sum_one_grad, weight_in)


def row_mean(x):
    return jnp.mean(x, axis=-1, keepdims=True)


def col_sum(x):
    return jnp.sum(x, axis=0, keepdims=True)


def layer_norm(u, gain, shift):
    centred = u - row_mean(u)
    scale = lax.rsqrt(row_mean(centred * centred) + EPS_NORM)
    hat = centred * scale
    return hat, scale, hat * gain + shift


def layer_norm_grad(hat, scale, gain, grad):
    gg = grad * gain
    return scale * (gg - row_mean(gg) - hat * row_mean(gg * hat))


def middle_kernel(
    ff,
    chunk,
    ctx_ref,
    hid_ref,
    og_ref,
    seg_ref,
    wo_ref,
    we_ref,
    wr_ref,
    down_ref,
    down_bias_ref,
    up_ref,
    up_bias_ref,
    gain_ref,
    shift_ref,
    out_ref,
    sog_ref,
    cg_ref,
    sums_ref,
    slope_ref,
    normed_ref,
    acc_ref,
):
    rank = up_ref.shape[1]
    small = 4 * rank

    @pl.when(pl.program_id(0) == 0)
    def _():
        sums_ref[...] = jnp.zeros_like(sums_ref)

    def adapter(k, a):
        a_low = a.astype(jnp.bfloat16)
        act, slope = gelu_pair(dot(a_low, down_ref[k]) + down_bias_ref[k : k + 1, :])
        act = act.astype(jnp.bfloat16)
        branch = dot(act, up_ref[k]) + up_bias_ref[k : k + 1, :]
        ratio = jnp.sqrt(row_mean(branch * branch)) / jnp.sqrt(row_mean(a * a) + EPS_RATIO)
        return branch, ratio, (a_low, act, slope)

    def add(row, value):
        sums_ref[row : row + 1, : value.shape[1]] += value

    def adapter_grad(k, kept, grad):
        a_low, act, slope = kept
        grad_low = grad.astype(jnp.bfloat16)
        hidden_grad = slope * dot_nt(grad_low, up_ref[k])
        hidden_grad = hidden_grad.astype(jnp.bfloat16)
        sums_ref[k * rank : (k + 1) * rank, :] += dot_tn(hidden_grad, a_low)
        sums_ref[(2 + k) * rank : (3 + k) * rank, :] += dot_tn(act, grad_low)
        add(small + k, col_sum(grad_low.astype(jnp.float32)))
        add(small + 6 + k, col_sum(hidden_grad.astype(jnp.float32)))
        return (grad + dot_nt(hidden_grad, down_ref[k])).astype(jnp.bfloat16)

    gain_one, gain_two = gain_ref[0:1, :], gain_ref[1:2, :]
    attended = dot(ctx_ref[...], wo_ref[...])
    branch, ratio_one, kept_one = adapter(0, attended)
    hat_one, scale_one, normed = layer_norm(
        hid_ref[...].astype(jnp.float32) + attended + branch, gain_one, shift_ref[0:1, :]
    )
    normed_ref[...] = normed.astype(jnp.bfloat16)
    acc_ref[...] = jnp.zeros_like(acc_ref)

    def feed(c, _):
        at = cols(c * chunk, chunk)
        act, slope = gelu_pair(dot(normed_ref[...], we_ref[:, at]))
        slope_ref[:, at] = slope
        acc_ref[...] += dot(act.astype(jnp.bfloat16), wr_ref[at, :])
        return 0

    lax.fori_loop(0, ff // chunk, feed, 0, unroll=2)
    feed_out = acc_ref[...]
    branch, ratio_two, kept_two = adapter(1, feed_out)
    hat_two, scale_two, final = layer_norm(normed + feed_out + branch, gain_two, shift_ref[1:2, :])
    out_ref[...] = final.astype(jnp.bfloat16)

    lane = lax.broadcasted_iota(jnp.int32, (1, 128), 1)
    ratios = jnp.where(lane == 0, ratio_one, jnp.where(lane == 1, ratio_two, 1.0))
    valid = (seg_ref[0] >= 0).astype(jnp.float32)
    stats = jnp.dot(
        jnp.broadcast_to(valid, (8, valid.shape[1])),
        ratios,
        precision=lax.Precision.HIGHEST,
        preferred_element_type=jnp.float32,
    )
    add(small + 8, stats[0:1, :])

    grad = og_ref[...].astype(jnp.float32)
    add(small + 3, col_sum(grad * hat_two))
    add(small + 5, col_sum(grad))
    sum_two_grad = layer_norm_grad(hat_two, scale_two, gain_two, grad)
    normed_ref[...] = adapter_grad(1, kept_two, sum_two_grad)
    acc_ref[...] = sum_two_grad

    def feed_grad(c, _):
        at = cols(c * chunk, chunk)
        inner_grad = slope_ref[:, at] * dot_nt(normed_ref[...], wr_ref[at, :])
        acc_ref[...] += dot_nt(inner_grad.astype(jnp.bfloat16), we_ref[:, at])
        return 0

    lax.fori_loop(0, ff // chunk, feed_grad, 0, unroll=2)
    grad = acc_ref[...]
    add(small + 2, col_sum(grad * hat_one))
    add(small + 4, col_sum(grad))
    sum_one_grad = layer_norm_grad(hat_one, scale_one, gain_one, grad)
    sog_ref[...] = sum_one_grad
    attended_grad = adapter_grad(0, kept_one, sum_one_grad)
    cg_ref[...] = dot_nt(attended_grad, wo_ref[...]).astype(jnp.bfloat16)


TILE = 256
CHUNK = 512
SUM_ROWS = 288


def middle(ctx, hidden, output_grad, seg_ids, frozen, params):
    rows, width = hidden.shape
    weight_out, weight_expand, weight_reduce = frozen
    ff = weight_expand.shape[1]
    seg_tiles = seg_ids.reshape(rows // TILE, 1, TILE)
    whole = [weight_out, weight_expand, weight_reduce, *params]

    def tile_spec(n):
        return pl.BlockSpec((TILE, n), lambda i: (i, 0))

    def whole_spec(x):
        return pl.BlockSpec(x.shape, lambda i: (0,) * x.ndim, pipeline_mode=pl.Buffered(1))

    return pl.pallas_call(
        lambda *refs: middle_kernel(ff, CHUNK, *refs),
        grid=(rows // TILE,),
        out_shape=[
            jax.ShapeDtypeStruct((rows, width), jnp.bfloat16),
            jax.ShapeDtypeStruct((rows, width), jnp.float32),
            jax.ShapeDtypeStruct((rows, width), jnp.bfloat16),
            jax.ShapeDtypeStruct((SUM_ROWS, width), jnp.float32),
        ],
        in_specs=[tile_spec(width)] * 3
        + [pl.BlockSpec((1, 1, TILE), lambda i: (i, 0, 0))]
        + [whole_spec(x) for x in whole],
        out_specs=[tile_spec(width)] * 3 + [pl.BlockSpec((SUM_ROWS, width), lambda i: (0, 0))],
        scratch_shapes=[
            pltpu.VMEM((TILE, ff), jnp.float32),
            pltpu.VMEM((TILE, width), jnp.bfloat16),
            pltpu.VMEM((TILE, width), jnp.float32),
        ],
        compiler_params=pltpu.CompilerParams(vmem_limit_bytes=VMEM_LIMIT),
        cost_estimate=pl.CostEstimate(
            flops=4 * rows * width * (width + 2 * ff),
            bytes_accessed=14 * rows * width + 2 * width * (width + 2 * ff),
            transcendentals=2 * rows * ff,
        ),
        name="middle",
    )(ctx, hidden, output_grad, seg_tiles, *whole)


def body(
    hidden_states,
    segment_ids,
    input_weight,
    output_weight,
    expand_weight,
    reduce_weight,
    adapter_down,
    adapter_down_bias,
    adapter_up,
    adapter_up_bias,
    norm_gain,
    norm_shift,
    output_grad,
):
    weight_in, *frozen = gather_weights(
        [input_weight, output_weight, expand_weight, reduce_weight]
    )
    rank = adapter_up.shape[1]
    seg_rows = segment_ids.reshape(-1, 1, SEQ_LEN)
    qkv, ctx = attend_forward(hidden_states, seg_rows, weight_in)
    params = (
        adapter_down,
        adapter_down_bias,
        adapter_up,
        adapter_up_bias,
        norm_gain,
        norm_shift,
    )
    output, sum_one_grad, ctx_grad, sums = middle(
        ctx, hidden_states, output_grad, segment_ids, frozen, params
    )
    sums = lax.psum(sums, ("dp", "head"))
    input_grad = attend_backward(qkv, ctx_grad, seg_rows, sum_one_grad, weight_in)
    small = 4 * rank
    stats = sums[small + 8]
    return (
        output,
        input_grad,
        stats[:2] / stats[2],
        jnp.transpose(sums[: 2 * rank].reshape(2, rank, -1), (0, 2, 1)),
        sums[small + 6 : small + 8, :rank],
        sums[2 * rank : small].reshape(2, rank, -1),
        sums[small : small + 2],
        sums[small + 2 : small + 4],
        sums[small + 4 : small + 6],
    )


def solution(mesh):
    tokens = P(("dp", "head"), None)
    in_specs = (tokens, P(("dp", "head"))) + (P("dp", None),) * 4 + (P(),) * 6 + (tokens,)
    out_specs = (tokens, tokens) + (P(),) * 7
    return jax.shard_map(body, mesh=mesh, in_specs=in_specs, out_specs=out_specs, check_vma=False)
```

profile of v0, /device:TPU:0, one launch (start us, length us, event | category | flops | bytes accessed | tf_op | source)
XLA Modules:
  0.0 333.0 jit_solution(16458868363219866573)
XLA Ops:
  7.2 0.0 all-reduce.2.cloned.1.call-start
  7.2 1.8 copy.22.refs_7_
  9.1 86.5 %gather_weights.1 = (bf16[16,48,2304]{2,1,0:T(8,128)(2,1)}, bf16[16,48,768]{2,1,0:T(8,128)(2,1)}, bf16[16,48,3072]{2,1,0:T(8,128)(2,1)}, bf16[16,192,768]{2,1,0:T(8,128)(2,1)}) custom-call(bf16[48,2304]{1,0:T(8,128)(2,1)} %refs_0_.2, bf16[48,768]{1,0:T(8,128)(2,1)} %refs_1_.2, bf16[48,3072]{1,0:T(8,128)(2,1)} %refs_2_.2, bf16[192,768]{1,0:T(8,128)(2,1)} %refs_3_.1), custom_call_target="tpu_custom_call" | custom-call | tf_op jit(solution)/shard_map/gather_weights/pallas_call | solution.py:172
  95.5 24.7 %attend_forward.1 = (bf16[1024,2304]{1,0:T(8,128)(2,1)}, bf16[1024,768]{1,0:T(8,128)(2,1)}) custom-call(bf16[1024,768]{1,0:T(8,128)(2,1)} %refs_1_.3, s32[2,1,512]{2,1,0:T(1,128)} %bitcast.20, bf16[768,2304]{1,0:T(8,128)(2,1)} %bitcast.17), custom_call_target="tpu_custom_call" | custom-call | flops 5234491392 | bytes 11403264 | tf_op jit(solution)/shard_map/attend_forward/pallas_call | solution.py:289
  120.2 66.1 %middle.1 = (bf16[1024,768]{1,0:T(8,128)(2,1)}, f32[1024,768]{1,0:T(8,128)}, bf16[1024,768]{1,0:T(8,128)(2,1)}, f32[288,768]{1,0:T(8,128)}) custom-call(bf16[1024,768]{1,0:T(8,128)(2,1)} %get-tuple-element.20.refs_0_, bf16[1024,768]{1,0:T(8,128)(2,1)} %refs_1_.3, bf16[1024,768]{1,0:T(8,128)(2,1)} %refs_2_.3, s32[4,1,256]{2,1,0:T(1,128)} %bitcast.21, ...), custom_call_target="tpu_custom_call" | custom-call | flops 21743271936 | bytes 21626880 | tf_op jit(solution)/shard_map/middle/pallas_call | solution.py:524
  186.3 0.0 all-reduce.2.cloned.1.call-update
  186.3 39.4 %attend_backward.1 = f32[1024,768]{1,0:T(8,128)} custom-call(bf16[1024,2304]{1,0:T(8,128)(2,1)} %get-tuple-element.25.refs_0_, bf16[1024,768]{1,0:T(8,128)(2,1)} %get-tuple-element.26.refs_1_, s32[2,1,512]{2,1,0:T(1,128)} %bitcast.22, f32[1024,768]{1,0:T(8,128)} %get-tuple-element.27.refs_3_, bf16[768,2304]{1,0:T(8,128)(2,1)} %bitcast.18), custom_call_target="tpu_custom_call" | custom-call | flops 7650410496 | bytes 16121856 | tf_op jit(solution)/shard_map/attend_backward/pallas_call | solution.py:351
  225.7 92.7 %all-reduce.2.cloned.1.call-done = f32[288,768]{1,0:T(8,128)} async-done(((f32[288,768]{1,0:T(8,128)}), f32[288,768]{1,0:T(8,128)}) %all-reduce.2.cloned.1.call-update) | async-done | bytes 884752 | tf_op jit(solution)/shard_map/psum | solution.py:584
  318.4 1.2 slice.38
  319.6 1.2 slice.40
  320.9 1.5 fusion.1
  322.3 2.0 fusion.2
  324.4 1.7 fusion
Async XLA Ops:
  7.2 311.2 %all-reduce.2.cloned.1.call-start = ((), (), s32[]{:S(2)}) async-start(), calls=%async_computation | async-start | bytes 1769472 | tf_op jit(solution)/shard_map/psum | solution.py:584
Sparse Core Ops, SparseCore 0:
  186.4 131.9 all-reduce.1
where the time goes:
time: 333 us
  Pallas kernels  217 us (65%)
  waiting for transfers between devices  92.8 us (28%)
  between operations  14.1 us (4%)
  local copies, waits for them, and re-layouts  7.83 us (2%)
    psum x1, waiting for transfers between devices, body(): sums = lax.psum(sums, ('dp', 'head'))  92.7 us
    pallas_call x1, Pallas kernels, gather_weights(): pl.pallas_call(lambda *refs: gather_kernel(depth, *refs), out_shape=[jax....  86.5 us
    pallas_call x1, Pallas kernels, middle(): pl.pallas_call(lambda *refs: middle_kernel(ff, CHUNK, *refs), grid=(rows...  66.1 us
    pallas_call x1, Pallas kernels, attend_backward(): pl.pallas_call(lambda *refs: attend_grad_kernel(width, *refs), grid=(rows...  39.4 us
    pallas_call x1, Pallas kernels, attend_forward(): pl.pallas_call(lambda *refs: attend_kernel(width, *refs), grid=(seqs,), o...  24.7 us
  transfers between devices with their start and end apart: 1, of which 1 were waited for; matrix products, arithmetic and copies ran while one was open for 0% of the time, Pallas kernels for 12%

commit v1 on v0

--- a/solution.py
+++ b/solution.py
@@ -313,11 +313,134 @@
     )(hidden, seg_rows, weight_in)
 
 
-def attend_grad_kernel(width, qkv_ref, cg_ref, seg_ref, sog_ref, w_ref, out_ref, grad_ref, bias_ref):
+def reduce_phases(depth, sums_ref, out_ref, first, second, third, fourth, acc, total, send_sem, recv_sem):
+    me = lax.axis_index("dp")
+    core = lax.axis_index("head")
+    z = me // PLANE
+    step_a, step_b = 1 + core, 2 - core
+    a, b = (me // step_a) % 2, (me // step_b) % 2
+    peer_a = {"dp": z * PLANE + (1 - a) * step_a + b * step_b}
+    peer_b = {"dp": z * PLANE + a * step_a + (1 - b) * step_b}
+    partner = {"head": 1 - core}
+    ring = [{"dp": (z + d) % depth * PLANE + me % PLANE} for d in range(1, depth)]
+    half = sums_ref.shape[0] // 2
+    quarter, eighth = half // 2, half // 4
+    piece = eighth // depth
+
+    def rows(start, size):
+        return pl.ds(pl.multiple_of(start, 8), size)
+
+    def send(slot, src, dst, target):
+        copy = pltpu.make_async_remote_copy(
+            src_ref=src,
+            dst_ref=dst,
+            send_sem=send_sem.at[slot],
+            recv_sem=recv_sem.at[slot],
+            device_id=target,
+            device_id_type=MESH,
+        )
+        copy.start()
+
+    def wait(sem, view):
+        pltpu.make_async_copy(view, view, sem).wait()
+
+    def arrive(slot, view):
+        wait(recv_sem.at[slot], view)
+        return view
+
+    base_a = core * half + a * quarter
+    base_b = base_a + b * eighth
+    local_b = a * quarter + b * eighth
+    one, two, three, back_b, back_a, back = range(6)
+    out_z = [6 + d for d in range(depth - 1)]
+    back_z = [5 + depth + d for d in range(depth - 1)]
+
+    def start():
+        barrier = pltpu.get_barrier_semaphore()
+        for target in [partner, peer_a, peer_b] + ring:
+            pl.semaphore_signal(barrier, inc=1, device_id=target, device_id_type=MESH)
+        pl.semaphore_wait(barrier, 2 + depth)
+        send(one, sums_ref.at[rows((1 - core) * half, half), :], first, partner)
+
+    def reduce_a():
+        arrive(one, first)
+        acc[...] = sums_ref[rows(core * half, half), :] + first[...]
+        send(two, acc.at[rows((1 - a) * quarter, quarter), :], second, peer_a)
+
+    def reduce_b():
+        arrive(two, second)
+        acc[rows(a * quarter, quarter), :] += second[...]
+        send(three, acc.at[rows(a * quarter + (1 - b) * eighth, eighth), :], third, peer_b)
+
+    def reduce_z():
+        arrive(three, third)
+        acc[rows(local_b, eighth), :] += third[...]
+        for d in range(depth - 1):
+            owner = (z + 1 + d) % depth
+            src = acc.at[rows(local_b + owner * piece, piece), :]
+            send(out_z[d], src, fourth.at[d], ring[d])
+
+    def finish():
+        mine = acc[rows(local_b + z * piece, piece), :]
+        for d in range(depth - 1):
+            arrive(out_z[d], fourth.at[d])
+            mine += fourth[d]
+        view = total.at[rows(base_b + z * piece, piece), :]
+        view[...] = mine
+        for d in range(depth - 1):
+            send(back_z[d], view, view, ring[d])
+
+    def return_b():
+        for d in range(depth - 1):
+            sender = (z + depth - 1 - d) % depth
+            arrive(back_z[d], total.at[rows(base_b + sender * piece, piece), :])
+        view = total.at[rows(base_b, eighth), :]
+        send(back_b, view, view, peer_b)
+
+    def return_a():
+        arrive(back_b, total.at[rows(base_a + (1 - b) * eighth, eighth), :])
+        view = total.at[rows(base_a, quarter), :]
+        send(back_a, view, view, peer_a)
+
+    def return_core():
+        arrive(back_a, total.at[rows(core * half + (1 - a) * quarter, quarter), :])
+        view = total.at[rows(core * half, half), :]
+        send(back, view, view, partner)
+
+    def end():
+        arrive(back, total.at[rows((1 - core) * half, half), :])
+        out_ref[...] = total[...]
+        for slot, view in [
+            (one, first),
+            (two, second),
+            (three, third),
+            (back_b, third),
+            (back_a, second),
+            (back, first),
+        ]:
+            wait(send_sem.at[slot], view)
+        for slot in out_z + back_z:
+            wait(send_sem.at[slot], fourth.at[0])
+
+    return [start, reduce_a, reduce_b, reduce_z, finish, return_b, return_a, return_core, end]
+
+
+def attend_grad_kernel(width, depth, *refs):
+    qkv_ref, cg_ref, seg_ref, sog_ref, w_ref = refs[:5]
+    if depth:
+        sums_ref, out_ref, reduced_ref, grad_ref, bias_ref = refs[5:10]
+        *phases, end = reduce_phases(depth, sums_ref, reduced_ref, *refs[10:])
+    else:
+        out_ref, grad_ref, bias_ref = refs[5:]
+        phases = []
+    turn = pl.program_id(0)
+    pairs = width // PAIR
     bias_ref[...] = score_bias(seg_ref[0])
     low, masks = head_lanes()
 
     def pair(h, _):
+        for n, phase in enumerate(phases):
+            pl.when(turn * pairs + h == n)(phase)
         q = qkv_ref[:, cols(h * PAIR, PAIR)]
         k = qkv_ref[:, cols(width + h * PAIR, PAIR)]
         v = qkv_ref[:, cols(2 * width + h * PAIR, PAIR)]
@@ -335,7 +458,7 @@
             grad_ref[:, cols(n * width + h * PAIR, PAIR)] = both.astype(jnp.bfloat16)
         return 0
 
-    lax.fori_loop(0, width // PAIR, pair, 0)
+    lax.fori_loop(0, pairs, pair, 0)
     step = 256
 
     def back(c, _):
@@ -344,34 +467,95 @@
         return 0
 
     lax.fori_loop(0, width // step, back, 0)
-
-
-def attend_backward(qkv, ctx_grad, seg_rows, sum_one_grad, weight_in):
+    if phases:
+        pl.when(turn == pl.num_programs(0) - 1)(end)
+
+
+def attend_backward(qkv, ctx_grad, seg_rows, sum_one_grad, weight_in, sums):
     rows, width = ctx_grad.shape
-    return pl.pallas_call(
-        lambda *refs: attend_grad_kernel(width, *refs),
+    count, span = sums.shape
+    size = lax.axis_size("dp")
+    depth = size // PLANE
+    fits = size % PLANE == 0 and count % (64 * depth) == 0 and rows // SEQ_LEN * (width // PAIR) >= 8
+    fits = fits and depth > 1
+    if not fits:
+        depth = 0
+    operands = [qkv, ctx_grad, seg_rows, sum_one_grad, weight_in]
+    in_specs = [
+        pl.BlockSpec((SEQ_LEN, 3 * width), lambda i: (i, 0)),
+        pl.BlockSpec((SEQ_LEN, width), lambda i: (i, 0)),
+        pl.BlockSpec((1, 1, SEQ_LEN), lambda i: (i, 0, 0)),
+        pl.BlockSpec((SEQ_LEN, width), lambda i: (i, 0)),
+        pl.BlockSpec((width, 3 * width), lambda i: (0, 0)),
+    ]
+    out_shape = [jax.ShapeDtypeStruct((rows, width), jnp.float32)]
+    out_specs = [pl.BlockSpec((SEQ_LEN, width), lambda i: (i, 0))]
+    scratch = [
+        pltpu.VMEM((SEQ_LEN, 3 * width), jnp.bfloat16),
+        pltpu.VMEM((SEQ_LEN, SEQ_LEN), jnp.float32),
+    ]
+    settings = {"vmem_limit_bytes": VMEM_LIMIT}
+    if fits:
+        operands.append(sums)
+        in_specs.append(pl.BlockSpec((count, span), lambda i: (0, 0)))
+        out_shape.append(jax.ShapeDtypeStruct((count, span), jnp.float32))
+        out_specs.append(pl.BlockSpec((count, span), lambda i: (0, 0)))
+        scratch += [
+            pltpu.VMEM((count // 2, span), jnp.float32),
+            pltpu.VMEM((count // 4, span), jnp.float32),
+            pltpu.VMEM((count // 8, span), jnp.float32),
+            pltpu.VMEM((depth - 1, count // 8 // depth, span), jnp.float32),
+            pltpu.VMEM((count // 2, span), jnp.float32),
+            pltpu.VMEM((count, span), jnp.float32),
+            pltpu.SemaphoreType.DMA((4 + 2 * depth,)),
+            pltpu.SemaphoreType.DMA((4 + 2 * depth,)),
+        ]
+        settings |= {"collective_id": 1, "has_side_effects": True}
+    input_grad, *reduced = pl.pallas_call(
+        lambda *refs: attend_grad_kernel(width, depth, *refs),
         grid=(rows // SEQ_LEN,),
-        out_shape=jax.ShapeDtypeStruct((rows, width), jnp.float32),
-        in_specs=[
-            pl.BlockSpec((SEQ_LEN, 3 * width), lambda i: (i, 0)),
-            pl.BlockSpec((SEQ_LEN, width), lambda i: (i, 0)),
-            pl.BlockSpec((1, 1, SEQ_LEN), lambda i: (i, 0, 0)),
-            pl.BlockSpec((SEQ_LEN, width), lambda i: (i, 0)),
-            pl.BlockSpec((width, 3 * width), lambda i: (0, 0)),
-        ],
-        out_specs=pl.BlockSpec((SEQ_LEN, width), lambda i: (i, 0)),
-        scratch_shapes=[
-            pltpu.VMEM((SEQ_LEN, 3 * width), jnp.bfloat16),
-            pltpu.VMEM((SEQ_LEN, SEQ_LEN), jnp.float32),
-        ],
-        compiler_params=pltpu.CompilerParams(vmem_limit_bytes=VMEM_LIMIT),
+        out_shape=out_shape,
+        in_specs=in_specs,
+        out_specs=out_specs,
+        scratch_shapes=scratch,
+        compiler_params=pltpu.CompilerParams(**settings),
         cost_estimate=pl.CostEstimate(
             flops=rows * width * (6 * width + 10 * SEQ_LEN),
             bytes_accessed=2 * rows * 8 * width + 6 * width * width,
             transcendentals=rows * SEQ_LEN * width // HEAD_DIM,
         ),
         name="attend_backward",
-    )(qkv, ctx_grad, seg_rows, sum_one_grad, weight_in)
+    )(*operands)
+    return input_grad, reduced[0] if fits else lax.psum(sums, ("dp", "head"))
+
+
+def unpack_kernel(sums_ref, ratio_ref, down_ref, down_bias_ref, up_ref, up_bias_ref, gain_ref, shift_ref):
+    rank, width = up_ref.shape[1:]
+    tall = sums_ref[: 2 * rank, :width].T
+    for k in range(2):
+        down_ref[k] = tall[:, k * rank : (k + 1) * rank]
+        up_ref[k] = sums_ref[(2 + k) * rank : (3 + k) * rank, :width]
+    for n in range(width // 128):
+        at = slice(128 * n, 128 * n + 128)
+        tile = sums_ref[8 * n : 8 * n + 8, width:]
+        up_bias_ref[:, at] = tile[0:2]
+        gain_ref[:, at] = tile[2:4]
+        shift_ref[:, at] = tile[4:6]
+        if n == 0:
+            down_bias_ref[...] = tile[6:8, :rank]
+        if n == 1:
+            ratio_ref[...] = tile[6:7, 0:2] / tile[6:7, 2:3]
+
+
+def unpack(sums, rank):
+    width = sums.shape[1] - 128
+    shapes = [(1, 2), (2, width, rank), (2, rank), (2, rank, width)] + [(2, width)] * 3
+    ratio, *rest = pl.pallas_call(
+        unpack_kernel,
+        out_shape=[jax.ShapeDtypeStruct(shape, jnp.float32) for shape in shapes],
+        name="unpack",
+    )(sums)
+    return (ratio.reshape(2), *rest)
 
 
 def row_mean(x):
@@ -414,16 +598,18 @@
     sog_ref,
     cg_ref,
     sums_ref,
+    small_ref,
     slope_ref,
     normed_ref,
     acc_ref,
 ):
     rank = up_ref.shape[1]
-    small = 4 * rank
+    width = up_ref.shape[2]
 
     @pl.when(pl.program_id(0) == 0)
     def _():
         sums_ref[...] = jnp.zeros_like(sums_ref)
+        small_ref[...] = jnp.zeros_like(small_ref)
 
     def adapter(k, a):
         a_low = a.astype(jnp.bfloat16)
@@ -433,18 +619,18 @@
         ratio = jnp.sqrt(row_mean(branch * branch)) / jnp.sqrt(row_mean(a * a) + EPS_RATIO)
         return branch, ratio, (a_low, act, slope)
 
-    def add(row, value):
-        sums_ref[row : row + 1, : value.shape[1]] += value
+    def add(row, value, start=0):
+        small_ref[row : row + 1, start : start + value.shape[1]] += value
 
     def adapter_grad(k, kept, grad):
         a_low, act, slope = kept
         grad_low = grad.astype(jnp.bfloat16)
         hidden_grad = slope * dot_nt(grad_low, up_ref[k])
         hidden_grad = hidden_grad.astype(jnp.bfloat16)
-        sums_ref[k * rank : (k + 1) * rank, :] += dot_tn(hidden_grad, a_low)
-        sums_ref[(2 + k) * rank : (3 + k) * rank, :] += dot_tn(act, grad_low)
-        add(small + k, col_sum(grad_low.astype(jnp.float32)))
-        add(small + 6 + k, col_sum(hidden_grad.astype(jnp.float32)))
+        sums_ref[k * rank : (k + 1) * rank, :width] += dot_tn(hidden_grad, a_low)
+        sums_ref[(2 + k) * rank : (3 + k) * rank, :width] += dot_tn(act, grad_low)
+        add(k, col_sum(grad_low.astype(jnp.float32)))
+        add(6 + k, col_sum(hidden_grad.astype(jnp.float32)))
         return (grad + dot_nt(hidden_grad, down_ref[k])).astype(jnp.bfloat16)
 
     gain_one, gain_two = gain_ref[0:1, :], gain_ref[1:2, :]
@@ -478,11 +664,11 @@
         precision=lax.Precision.HIGHEST,
         preferred_element_type=jnp.float32,
     )
-    add(small + 8, stats[0:1, :])
+    add(6, stats[0:1, :], 128)
 
     grad = og_ref[...].astype(jnp.float32)
-    add(small + 3, col_sum(grad * hat_two))
-    add(small + 5, col_sum(grad))
+    add(3, col_sum(grad * hat_two))
+    add(5, col_sum(grad))
     sum_two_grad = layer_norm_grad(hat_two, scale_two, gain_two, grad)
     normed_ref[...] = adapter_grad(1, kept_two, sum_two_grad)
     acc_ref[...] = sum_two_grad
@@ -495,17 +681,22 @@
 
     lax.fori_loop(0, ff // chunk, feed_grad, 0, unroll=2)
     grad = acc_ref[...]
-    add(small + 2, col_sum(grad * hat_one))
-    add(small + 4, col_sum(grad))
+    add(2, col_sum(grad * hat_one))
+    add(4, col_sum(grad))
     sum_one_grad = layer_norm_grad(hat_one, scale_one, gain_one, grad)
     sog_ref[...] = sum_one_grad
     attended_grad = adapter_grad(0, kept_one, sum_one_grad)
     cg_ref[...] = dot_nt(attended_grad, wo_ref[...]).astype(jnp.bfloat16)
 
+    @pl.when(pl.program_id(0) == pl.num_programs(0) - 1)
+    def _():
+        for n in range(width // 128):
+            sums_ref[8 * n : 8 * n + 8, width:] = small_ref[:, 128 * n : 128 * n + 128]
+
 
 TILE = 256
 CHUNK = 512
-SUM_ROWS = 288
+SUM_ROWS = 256
 
 
 def middle(ctx, hidden, output_grad, seg_ids, frozen, params):
@@ -528,13 +719,14 @@
             jax.ShapeDtypeStruct((rows, width), jnp.bfloat16),
             jax.ShapeDtypeStruct((rows, width), jnp.float32),
             jax.ShapeDtypeStruct((rows, width), jnp.bfloat16),
-            jax.ShapeDtypeStruct((SUM_ROWS, width), jnp.float32),
+            jax.ShapeDtypeStruct((SUM_ROWS, width + 128), jnp.float32),
         ],
         in_specs=[tile_spec(width)] * 3
         + [pl.BlockSpec((1, 1, TILE), lambda i: (i, 0, 0))]
         + [whole_spec(x) for x in whole],
-        out_specs=[tile_spec(width)] * 3 + [pl.BlockSpec((SUM_ROWS, width), lambda i: (0, 0))],
+        out_specs=[tile_spec(width)] * 3 + [pl.BlockSpec((SUM_ROWS, width + 128), lambda i: (0, 0))],
         scratch_shapes=[
+            pltpu.VMEM((8, width), jnp.float32),
             pltpu.VMEM((TILE, ff), jnp.float32),
             pltpu.VMEM((TILE, width), jnp.bfloat16),
             pltpu.VMEM((TILE, width), jnp.float32),
@@ -567,7 +759,6 @@
     weight_in, *frozen = gather_weights(
         [input_weight, output_weight, expand_weight, reduce_weight]
     )
-    rank = adapter_up.shape[1]
     seg_rows = segment_ids.reshape(-1, 1, SEQ_LEN)
     qkv, ctx = attend_forward(hidden_states, seg_rows, weight_in)
     params = (
@@ -581,21 +772,8 @@
     output, sum_one_grad, ctx_grad, sums = middle(
         ctx, hidden_states, output_grad, segment_ids, frozen, params
     )
-    sums = lax.psum(sums, ("dp", "head"))
-    input_grad = attend_backward(qkv, ctx_grad, seg_rows, sum_one_grad, weight_in)
-    small = 4 * rank
-    stats = sums[small + 8]
-    return (
-        output,
-        input_grad,
-        stats[:2] / stats[2],
-        jnp.transpose(sums[: 2 * rank].reshape(2, rank, -1), (0, 2, 1)),
-        sums[small + 6 : small + 8, :rank],
-        sums[2 * rank : small].reshape(2, rank, -1),
-        sums[small : small + 2],
-        sums[small + 2 : small + 4],
-        sums[small + 4 : small + 6],
-    )
+    input_grad, sums = attend_backward(qkv, ctx_grad, seg_rows, sum_one_grad, weight_in, sums)
+    return (output, input_grad, *unpack(sums, adapter_up.shape[1]))
 
 
 def solution(mesh):

time: 333 us -> 246 us (0.74)
  waiting for transfers between devices: 92.8 us -> 0 us
  Pallas kernels: 217 us -> 237 us
  between operations: 14.1 us -> 0.67 us
    psum x1 -> x0, waiting for transfers between devices: 92.7 us -> none  [body(): sums = lax.psum(sums, ('dp', 'head'))]
    pallas_call x1 -> x2, Pallas kernels: 39.4 us -> 59.2 us  [the longest x1 56.8 us: attend_backward(): pl.pallas_call(lambda *refs: attend_grad_kernel(width, depth, *refs), gri...]
    slice x4 -> x0, local copies, waits for them, and re-layouts: 5.99 us -> none  [the longest x1 2.04 us: body(): sums[2 * rank:small].reshape(2, rank, -1)]
    unnamed x1 -> x3, local copies, waits for them, and re-layouts: 1.85 us -> 7.73 us
  transfers between devices with their start and end apart: 1 -> 0, of which waited for: 1 -> 0; matrix products, arithmetic and copies ran while one was open for 0% -> 0% of each run, Pallas kernels for 12% -> 0%
where the time goes in v1:
time: 246 us
  Pallas kernels  237 us (96%)
  local copies, waits for them, and re-layouts  7.73 us (3%)
    pallas_call x1, Pallas kernels, gather_weights(): pl.pallas_call(lambda *refs: gather_kernel(depth, *refs), out_shape=[jax....  86.5 us
    pallas_call x1, Pallas kernels, middle(): pl.pallas_call(lambda *refs: middle_kernel(ff, CHUNK, *refs), grid=(rows...  67.1 us
    pallas_call x1, Pallas kernels, attend_backward(): pl.pallas_call(lambda *refs: attend_grad_kernel(width, depth, *refs), gri...  56.8 us
    pallas_call x1, Pallas kernels, attend_forward(): pl.pallas_call(lambda *refs: attend_kernel(width, *refs), grid=(seqs,), o...  24.7 us
    unnamed x3, local copies, waits for them, and re-layouts  7.73 us

profile of v1, /device:TPU:0, one launch (start us, length us, event | category | flops | bytes accessed | tf_op | source)
XLA Modules:
  0.0 245.9 jit_solution(16403640510494137894)
XLA Ops:
  0.6 1.8 copy.22.refs_7_
  2.5 86.5 %gather_weights.1 = (bf16[16,48,2304]{2,1,0:T(8,128)(2,1)}, bf16[16,48,768]{2,1,0:T(8,128)(2,1)}, bf16[16,48,3072]{2,1,0:T(8,128)(2,1)}, bf16[16,192,768]{2,1,0:T(8,128)(2,1)}) custom-call(bf16[48,2304]{1,0:T(8,128)(2,1)} %refs_0_.2, bf16[48,768]{1,0:T(8,128)(2,1)} %refs_1_.2, bf16[48,3072]{1,0:T(8,128)(2,1)} %refs_2_.2, bf16[192,768]{1,0:T(8,128)(2,1)} %refs_3_.1), custom_call_target="tpu_custom_call" | custom-call | tf_op jit(solution)/shard_map/gather_weights/pallas_call | solution.py:172
  89.0 24.7 %attend_forward.1 = (bf16[1024,2304]{1,0:T(8,128)(2,1)}, bf16[1024,768]{1,0:T(8,128)(2,1)}) custom-call(bf16[1024,768]{1,0:T(8,128)(2,1)} %refs_1_.3, s32[2,1,512]{2,1,0:T(1,128)} %bitcast.12, bf16[768,2304]{1,0:T(8,128)(2,1)} %bitcast.9), custom_call_target="tpu_custom_call" | custom-call | flops 5234491392 | bytes 11403264 | tf_op jit(solution)/shard_map/attend_forward/pallas_call | solution.py:289
  113.7 67.1 %middle.1 = (bf16[1024,768]{1,0:T(8,128)(2,1)}, f32[1024,768]{1,0:T(8,128)}, bf16[1024,768]{1,0:T(8,128)(2,1)}, f32[256,896]{1,0:T(8,128)}) custom-call(bf16[1024,768]{1,0:T(8,128)(2,1)} %get-tuple-element.29.refs_0_, bf16[1024,768]{1,0:T(8,128)(2,1)} %refs_1_.3, bf16[1024,768]{1,0:T(8,128)(2,1)} %refs_2_.3, s32[4,1,256]{2,1,0:T(1,128)} %bitcast.13, ...), custom_call_target="tpu_custom_call" | custom-call | flops 21743271936 | bytes 21626880 | tf_op jit(solution)/shard_map/middle/pallas_call | solution.py:715
  180.8 56.8 %attend_backward.1 = (f32[1024,768]{1,0:T(8,128)}, f32[256,896]{1,0:T(8,128)}) custom-call(bf16[1024,2304]{1,0:T(8,128)(2,1)} %get-tuple-element.34.refs_0_, bf16[1024,768]{1,0:T(8,128)(2,1)} %get-tuple-element.35.refs_1_, s32[2,1,512]{2,1,0:T(1,128)} %bitcast.14, f32[1024,768]{1,0:T(8,128)} %get-tuple-element.36.refs_3_, bf16[768,2304]{1,0:T(8,128)(2,1)} %bitcast.10, ...), custom_call_target="tpu_custom_call" | custom-call | flops 7650410496 | bytes 16121856 | tf_op jit(solution)/shard_map/attend_backward/pallas_call | solution.py:514
  237.5 2.4 unpack.1
  240.0 2.1 copy.23
  242.1 3.8 %copy.25 = f32[1024,768]{1,0:T(8,128)} copy(f32[1024,768]{1,0:T(8,128)} %get-tuple-element.66) | data formatting | bytes 6291456

commit v2 on v1

--- a/solution.py
+++ b/solution.py
@@ -9,9 +9,7 @@
 PLANE = 4
 
 
-def gather_kernel(depth, *refs):
-    shards, outs = refs[:4], refs[4:8]
-    own_sem, send_sem, recv_sem, pair_send, pair_recv = refs[8:]
+def gather_stages(depth, z_first, shards, outs, own_sem, send_sem, recv_sem, pair_send, pair_recv):
     me = lax.axis_index("dp")
     core = lax.axis_index("head")
     z = me // PLANE
@@ -22,169 +20,217 @@
     peer_a = z * PLANE + (1 - a) * step_a + b * step_b
     peer_b = z * PLANE + a * step_a + (1 - b) * step_b
     up, down = me + PLANE, me - PLANE
-    has_up, has_down = z < depth - 1, z > 0
     partner = 1 - core
+
+    def has_up():
+        return z < depth - 1
+
+    def has_down():
+        return z > 0
+
+    count = len(outs)
+    pending = []
 
     def owner(z_of, a_of, b_of):
         return z_of * PLANE + a_of * step_a + b_of * step_b
-
-    barrier = pltpu.get_barrier_semaphore()
-
-    def greet(cond, target):
-        def signal():
-            pl.semaphore_signal(barrier, inc=1, device_id=target, device_id_type=MESH)
-
-        if cond is None:
-            signal()
-        else:
-            pl.when(cond)(signal)
-
-    greet(None, {"dp": peer_a})
-    greet(None, {"dp": peer_b})
-    greet(None, {"head": partner})
-    greet(has_up, {"dp": up})
-    greet(has_down, {"dp": down})
-    pl.semaphore_wait(barrier, 3 + has_up.astype(jnp.int32) + has_down.astype(jnp.int32))
-
-    pending = []
 
     def guarded(cond, act):
         if cond is None:
             act()
         else:
-            pl.when(cond)(act)
+            pl.when(cond())(act)
 
     def send(cond, w, piece, src, dst, direction, slot, target):
-        copy = pltpu.make_async_remote_copy(
-            src_ref=src,
-            dst_ref=dst,
-            send_sem=send_sem.at[w, direction, slot],
-            recv_sem=recv_sem.at[w, piece],
-            device_id=target,
-            device_id_type=MESH,
-        )
-        guarded(cond, copy.start)
-        pending.append((cond, copy))
+        def copy():
+            return pltpu.make_async_remote_copy(
+                src_ref=src,
+                dst_ref=dst,
+                send_sem=send_sem.at[w, direction, slot],
+                recv_sem=recv_sem.at[w, piece],
+                device_id={"dp": target},
+                device_id_type=MESH,
+            )
+
+        guarded(cond, lambda: copy().start())
+        pending.append((cond, w, send_sem, (w, direction, slot)))
 
     def hand(cond, w, piece, view):
-        copy = pltpu.make_async_remote_copy(
-            src_ref=view,
-            dst_ref=view,
-            send_sem=pair_send.at[w, piece],
-            recv_sem=pair_recv.at[w, piece],
-            device_id={"head": partner},
-            device_id_type=MESH,
-        )
-        guarded(cond, copy.start)
-        pending.append((cond, copy))
-
-    def both(x, y):
-        return y if x is None else (x if y is None else jnp.logical_and(x, y))
-
-    def view_of(w, piece):
+        def copy():
+            return pltpu.make_async_remote_copy(
+                src_ref=view,
+                dst_ref=view,
+                send_sem=pair_send.at[w, piece],
+                recv_sem=pair_recv.at[w, piece],
+                device_id={"head": partner},
+                device_id_type=MESH,
+            )
+
+        guarded(cond, lambda: copy().start())
+
+    def view_of(w, piece, side):
         half = outs[w].shape[2] // 2
-        return outs[w].at[piece, :, pl.ds(pl.multiple_of(core * half, 128), half)]
+        return outs[w].at[piece, :, pl.ds(pl.multiple_of(side * half, 128), half)]
+
+    def wait(sem, view):
+        pltpu.make_async_copy(view, view, sem).wait()
 
     def arrive(cond, w, piece):
-        view = view_of(w, piece)
-
-        def wait():
-            pltpu.make_async_copy(view, view, recv_sem.at[w, piece]).wait()
-
-        guarded(cond, wait)
+        view = view_of(w, piece, core)
+        guarded(cond, lambda: wait(recv_sem.at[w, piece], view))
         return view
 
-    def start_own(w):
-        half = outs[w].shape[2] // 2
-        src = shards[w].at[:, pl.ds(pl.multiple_of(core * half, 128), half)]
-        view = view_of(w, me)
-        send(None, w, me, src, view, 0, 0, {"dp": peer_a})
-        send(has_up, w, me, src, view, 1, 0, {"dp": up})
-        send(has_down, w, me, src, view, 2, 0, {"dp": down})
-        send(None, w, me, src, view, 3, 0, {"dp": peer_b})
-        pltpu.make_async_copy(shards[w], outs[w].at[me], own_sem.at[w]).start()
+    def start():
+        barrier = pltpu.get_barrier_semaphore()
+
+        def greet(cond, target):
+            guarded(
+                cond,
+                lambda: pl.semaphore_signal(
+                    barrier, inc=1, device_id=target, device_id_type=MESH
+                ),
+            )
+
+        greet(None, {"dp": peer_a})
+        greet(None, {"dp": peer_b})
+        greet(None, {"head": partner})
+        greet(has_up, {"dp": up})
+        greet(has_down, {"dp": down})
+        pl.semaphore_wait(barrier, 3 + has_up().astype(jnp.int32) + has_down().astype(jnp.int32))
+        for w in range(count):
+            half = outs[w].shape[2] // 2
+            src = shards[w].at[:, pl.ds(pl.multiple_of(core * half, 128), half)]
+            view = view_of(w, me, core)
+            send(None, w, me, src, view, 0, 0, peer_a)
+            send(has_up, w, me, src, view, 1, 0, up)
+            send(has_down, w, me, src, view, 2, 0, down)
+            send(None, w, me, src, view, 3, 0, peer_b)
+        for w in range(count):
+            pltpu.make_async_copy(shards[w], outs[w].at[me], own_sem.at[w]).start()
 
     def first(w):
-        piece = peer_a
-        view = arrive(None, w, piece)
-        send(has_up, w, piece, view, view, 1, 1, {"dp": up})
-        send(has_down, w, piece, view, view, 2, 1, {"dp": down})
-        send(None, w, piece, view, view, 3, 1, {"dp": peer_b})
-        hand(None, w, piece, view)
+        if z_first[w]:
+            return
+        view = arrive(None, w, peer_a)
+        send(has_up, w, peer_a, view, view, 1, 1, up)
+        send(has_down, w, peer_a, view, view, 2, 1, down)
+        send(None, w, peer_a, view, view, 3, 1, peer_b)
+        hand(None, w, peer_a, view)
 
     def line(w, dist):
-        for k, a_of in enumerate((a, 1 - a)):
+        for k, a_of in enumerate((a,) if z_first[w] else (a, 1 - a)):
             slot = 2 * dist + k
-            below = z >= dist
-            piece = owner(z - dist, a_of, b)
-            view = arrive(below, w, piece)
-            send(both(below, has_up), w, piece, view, view, 1, slot, {"dp": up})
-            send(below, w, piece, view, view, 3, slot, {"dp": peer_b})
-            hand(below, w, piece, view)
-            above = z + dist < depth
-            piece = owner(z + dist, a_of, b)
-            view = arrive(above, w, piece)
-            send(both(above, has_down), w, piece, view, view, 2, slot, {"dp": down})
-            send(above, w, piece, view, view, 3, 2 * depth + slot, {"dp": peer_b})
-            hand(above, w, piece, view)
+            for above in (False, True):
+                z_of = z + dist if above else z - dist
+
+                def there(above=above):
+                    return z + dist < depth if above else z >= dist
+
+                def onward(above=above):
+                    inner = z > 0 if above else z < depth - 1
+                    return jnp.logical_and(there(above), inner)
+
+                piece = owner(z_of, a_of, b)
+                view = arrive(there, w, piece)
+                if above:
+                    send(onward, w, piece, view, view, 2, slot, down)
+                else:
+                    send(onward, w, piece, view, view, 1, slot, up)
+                late = 2 * depth * above + slot
+                if z_first[w]:
+                    send(there, w, piece, view, view, 0, late, peer_a)
+                send(there, w, piece, view, view, 3, late, peer_b)
+                hand(there, w, piece, view)
+
+    def across(w):
+        for z_of in range(depth):
+            piece = owner(z_of, 1 - a, b)
+            view = arrive(None, w, piece)
+            send(None, w, piece, view, view, 3, 4 * depth + z_of, peer_b)
+            hand(None, w, piece, view)
 
     def last(w):
         for z_of in range(depth):
             for a_of in range(2):
                 piece = owner(z_of, a_of, 1 - b)
-                view = arrive(None, w, piece)
-                hand(None, w, piece, view)
-
-    count = len(outs)
+                hand(None, w, piece, arrive(None, w, piece))
+
+    def finish():
+        for w in range(count):
+            wait(own_sem.at[w], outs[w].at[me])
+            for z_of in range(depth):
+                for a_of in range(2):
+                    for b_of in range(2):
+                        piece = owner(z_of, a_of, b_of)
+
+                        def pair(w=w, piece=piece):
+                            wait(pair_recv.at[w, piece], view_of(w, piece, partner))
+                            wait(pair_send.at[w, piece], view_of(w, piece, core))
+
+                        pl.when(piece != me)(pair)
+        for cond, w, sem, at in pending:
+            guarded(cond, lambda: wait(sem.at[at], view_of(w, me, core)))
+
+    def firsts():
+        for w in range(count):
+            first(w)
+
+    stages = [start, firsts]
+    for dist in range(1, depth):
+        for w in range(count):
+            stages.append(lambda w=w, dist=dist: line(w, dist))
     for w in range(count):
-        start_own(w)
-        first(w)
-        for dist in range(1, depth):
-            line(w, dist)
-            if w > 0 and dist == 1:
-                last(w - 1)
-    last(count - 1)
-
+        if z_first[w]:
+            stages.append(lambda w=w: across(w))
     for w in range(count):
-        pltpu.make_async_copy(shards[w], outs[w].at[me], own_sem.at[w]).wait()
-        half = outs[w].shape[2] // 2
-        for z_of in range(depth):
-            for a_of in range(2):
-                for b_of in range(2):
-                    piece = owner(z_of, a_of, b_of)
-                    other = pl.ds(pl.multiple_of((1 - core) * half, 128), half)
-
-                    def wait_pair(w=w, piece=piece, other=other):
-                        view = outs[w].at[piece, :, other]
-                        pltpu.make_async_copy(view, view, pair_recv.at[w, piece]).wait()
-
-                    pl.when(piece != me)(wait_pair)
-    for cond, copy in pending:
-        guarded(cond, copy.wait_send)
-
-
-def gather_weights(weights):
+        stages.append(lambda w=w: last(w))
+    return stages + [finish]
+
+
+def gather_scratch(count, size):
+    return [
+        pltpu.SemaphoreType.DMA((count,)),
+        pltpu.SemaphoreType.DMA((count, 4, 5 * (size // PLANE))),
+        pltpu.SemaphoreType.DMA((count, size)),
+        pltpu.SemaphoreType.DMA((count, size)),
+        pltpu.SemaphoreType.DMA((count, size)),
+    ]
+
+
+def gather_fits(weights):
     size = lax.axis_size("dp")
-    if size % PLANE or any(w.shape[0] % 16 or w.shape[1] % 256 for w in weights):
-        return [lax.all_gather(w, "dp", axis=0, tiled=True) for w in weights]
-    depth = size // PLANE
-    count = len(weights)
+    return (
+        size % PLANE == 0
+        and size > PLANE
+        and all(w.shape[0] % 16 == 0 and w.shape[1] % 256 == 0 for w in weights)
+    )
+
+
+def gather_shapes(weights):
+    size = lax.axis_size("dp")
+    return [jax.ShapeDtypeStruct((size,) + w.shape, w.dtype) for w in weights]
+
+
+def join(pieces):
+    return pieces.reshape(-1, pieces.shape[-1])
+
+
+def gather_kernel(depth, *refs):
+    for stage in gather_stages(depth, (False,), refs[:1], refs[1:2], *refs[2:]):
+        stage()
+
+
+def gather_first(weight):
+    size = lax.axis_size("dp")
     gathered = pl.pallas_call(
-        lambda *refs: gather_kernel(depth, *refs),
-        out_shape=[jax.ShapeDtypeStruct((size,) + w.shape, w.dtype) for w in weights],
-        in_specs=[pl.BlockSpec(memory_space=pltpu.VMEM)] * count,
-        out_specs=[pl.BlockSpec(memory_space=pl.ANY)] * count,
-        scratch_shapes=[
-            pltpu.SemaphoreType.DMA((count,)),
-            pltpu.SemaphoreType.DMA((count, 4, 4 * depth)),
-            pltpu.SemaphoreType.DMA((count, size)),
-            pltpu.SemaphoreType.DMA((count, size)),
-            pltpu.SemaphoreType.DMA((count, size)),
-        ],
+        lambda *refs: gather_kernel(size // PLANE, *refs),
+        out_shape=gather_shapes([weight]),
+        in_specs=[pl.BlockSpec(memory_space=pltpu.VMEM)],
+        out_specs=[pl.BlockSpec(memory_space=pl.ANY)],
+        scratch_shapes=gather_scratch(1, size),
         compiler_params=pltpu.CompilerParams(collective_id=0, has_side_effects=True),
-        name="gather_weights",
-    )(*weights)
-    return [g.reshape(size * w.shape[0], w.shape[1]) for g, w in zip(gathered, weights)]
+        name="gather_first",
+    )(weight)
+    return join(gathered[0])
 
 
 HEAD_DIM = 64
@@ -254,7 +300,17 @@
     return pl.ds(pl.multiple_of(start, 128), width)
 
 
-def attend_kernel(width, hid_ref, seg_ref, w_ref, qkv_ref, ctx_ref, bias_ref):
+def attend_kernel(width, depth, *refs):
+    hid_ref, seg_ref, w_ref = refs[:3]
+    if depth:
+        shards, (qkv_ref, ctx_ref), outs, bias_ref = refs[3:6], refs[6:8], refs[8:11], refs[11]
+        start, *stages, finish = gather_stages(depth, Z_FIRST, shards, outs, *refs[12:])
+        pl.when(pl.program_id(0) == 0)(start)
+    else:
+        qkv_ref, ctx_ref, bias_ref = refs[3:]
+        stages = []
+    turn = pl.program_id(0)
+    pairs = width // PAIR
     step = 256
 
     def project(c, _):
@@ -267,6 +323,8 @@
     low, masks = head_lanes()
 
     def pair(h, _):
+        for n, stage in enumerate(stages[: SLOTS]):
+            pl.when(turn * pairs + h == n)(stage)
         q = qkv_ref[:, cols(h * PAIR, PAIR)]
         k = qkv_ref[:, cols(width + h * PAIR, PAIR)]
         v = qkv_ref[:, cols(2 * width + h * PAIR, PAIR)]
@@ -280,37 +338,66 @@
         ctx_ref[:, cols(h * PAIR, PAIR)] = jnp.where(low, parts[0], parts[1]).astype(jnp.bfloat16)
         return 0
 
-    lax.fori_loop(0, width // PAIR, pair, 0)
-
-
-def attend_forward(hidden, seg_rows, weight_in):
+    lax.fori_loop(0, pairs, pair, 0)
+    if stages:
+
+        @pl.when(turn == pl.num_programs(0) - 1)
+        def _():
+            for stage in stages[SLOTS:]:
+                stage()
+            finish()
+
+
+Z_FIRST = (False, False, True)
+SLOTS = 12
+
+
+def attend_forward(hidden, seg_rows, weight_in, shards):
     rows, width = hidden.shape
-    seqs = rows // SEQ_LEN
-    return pl.pallas_call(
-        lambda *refs: attend_kernel(width, *refs),
-        grid=(seqs,),
-        out_shape=[
-            jax.ShapeDtypeStruct((rows, 3 * width), jnp.bfloat16),
-            jax.ShapeDtypeStruct((rows, width), jnp.bfloat16),
-        ],
-        in_specs=[
-            pl.BlockSpec((SEQ_LEN, width), lambda i: (i, 0)),
-            pl.BlockSpec((1, 1, SEQ_LEN), lambda i: (i, 0, 0)),
-            pl.BlockSpec((width, 3 * width), lambda i: (0, 0)),
-        ],
-        out_specs=[
-            pl.BlockSpec((SEQ_LEN, 3 * width), lambda i: (i, 0)),
-            pl.BlockSpec((SEQ_LEN, width), lambda i: (i, 0)),
-        ],
-        scratch_shapes=[pltpu.VMEM((SEQ_LEN, SEQ_LEN), jnp.float32)],
-        compiler_params=pltpu.CompilerParams(vmem_limit_bytes=VMEM_LIMIT),
+    size = lax.axis_size("dp")
+    fits = gather_fits(shards) and rows // SEQ_LEN * (width // PAIR) >= SLOTS
+    depth = size // PLANE if fits else 0
+    operands = [hidden, seg_rows, weight_in]
+    in_specs = [
+        pl.BlockSpec((SEQ_LEN, width), lambda i: (i, 0)),
+        pl.BlockSpec((1, 1, SEQ_LEN), lambda i: (i, 0, 0)),
+        pl.BlockSpec((width, 3 * width), lambda i: (0, 0)),
+    ]
+    out_shape = [
+        jax.ShapeDtypeStruct((rows, 3 * width), jnp.bfloat16),
+        jax.ShapeDtypeStruct((rows, width), jnp.bfloat16),
+    ]
+    out_specs = [
+        pl.BlockSpec((SEQ_LEN, 3 * width), lambda i: (i, 0)),
+        pl.BlockSpec((SEQ_LEN, width), lambda i: (i, 0)),
+    ]
+    scratch = [pltpu.VMEM((SEQ_LEN, SEQ_LEN), jnp.float32)]
+    settings = {"vmem_limit_bytes": VMEM_LIMIT}
+    if fits:
+        operands += shards
+        in_specs += [pl.BlockSpec(w.shape, lambda i: (0, 0)) for w in shards]
+        out_shape += gather_shapes(shards)
+        out_specs += [pl.BlockSpec(memory_space=pl.ANY)] * len(shards)
+        scratch += gather_scratch(len(shards), size)
+        settings |= {"collective_id": 2, "has_side_effects": True}
+    qkv, ctx, *gathered = pl.pallas_call(
+        lambda *refs: attend_kernel(width, depth, *refs),
+        grid=(rows // SEQ_LEN,),
+        out_shape=out_shape,
+        in_specs=in_specs,
+        out_specs=out_specs,
+        scratch_shapes=scratch,
+        compiler_params=pltpu.CompilerParams(**settings),
         cost_estimate=pl.CostEstimate(
             flops=rows * width * (6 * width + 4 * SEQ_LEN),
             bytes_accessed=2 * rows * 5 * width + 6 * width * width,
             transcendentals=rows * SEQ_LEN * width // HEAD_DIM,
         ),
         name="attend_forward",
-    )(hidden, seg_rows, weight_in)
+    )(*operands)
+    if not fits:
+        return qkv, ctx, [lax.all_gather(w, "dp", axis=0, tiled=True) for w in shards]
+    return qkv, ctx, [join(pieces) for pieces in gathered]
 
 
 def reduce_phases(depth, sums_ref, out_ref, first, second, third, fourth, acc, total, send_sem, recv_sem):
@@ -439,7 +526,7 @@
     low, masks = head_lanes()
 
     def pair(h, _):
-        for n, phase in enumerate(phases):
+        for n, phase in zip(REDUCE_SLOTS, phases):
             pl.when(turn * pairs + h == n)(phase)
         q = qkv_ref[:, cols(h * PAIR, PAIR)]
         k = qkv_ref[:, cols(width + h * PAIR, PAIR)]
@@ -471,12 +558,15 @@
         pl.when(turn == pl.num_programs(0) - 1)(end)
 
 
+REDUCE_SLOTS = (0, 1, 3, 4, 6, 8, 9, 11)
+
+
 def attend_backward(qkv, ctx_grad, seg_rows, sum_one_grad, weight_in, sums):
     rows, width = ctx_grad.shape
     count, span = sums.shape
     size = lax.axis_size("dp")
     depth = size // PLANE
-    fits = size % PLANE == 0 and count % (64 * depth) == 0 and rows // SEQ_LEN * (width // PAIR) >= 8
+    fits = size % PLANE == 0 and count % (64 * depth) == 0 and rows // SEQ_LEN * (width // PAIR) > REDUCE_SLOTS[-1]
     fits = fits and depth > 1
     if not fits:
         depth = 0
@@ -756,11 +846,13 @@
     norm_shift,
     output_grad,
 ):
-    weight_in, *frozen = gather_weights(
-        [input_weight, output_weight, expand_weight, reduce_weight]
-    )
+    if gather_fits([input_weight]):
+        weight_in = gather_first(input_weight)
+    else:
+        weight_in = lax.all_gather(input_weight, "dp", axis=0, tiled=True)
     seg_rows = segment_ids.reshape(-1, 1, SEQ_LEN)
-    qkv, ctx = attend_forward(hidden_states, seg_rows, weight_in)
+    shards = [output_weight, expand_weight, reduce_weight]
+    qkv, ctx, frozen = attend_forward(hidden_states, seg_rows, weight_in, shards)
     params = (
         adapter_down,
         adapter_down_bias,

time: 246 us -> 214 us (0.87)
  Pallas kernels: 237 us -> 206 us
    pallas_call x2, Pallas kernels: 111 us -> 86 us  [the longest x1 56.7 us: attend_forward(): pl.pallas_call(lambda *refs: attend_kernel(width, depth, *refs), grid=(ro...]
    pallas_call x1, Pallas kernels: 56.8 us -> 50 us  [attend_backward(): pl.pallas_call(lambda *refs: attend_grad_kernel(width, depth, *refs), gri...]
where the time goes in v2:
time: 214 us
  Pallas kernels  206 us (96%)
  local copies, waits for them, and re-layouts  7.73 us (4%)
    pallas_call x1, Pallas kernels, middle(): pl.pallas_call(lambda *refs: middle_kernel(ff, CHUNK, *refs), grid=(rows...  67.1 us
    pallas_call x1, Pallas kernels, attend_forward(): pl.pallas_call(lambda *refs: attend_kernel(width, depth, *refs), grid=(ro...  56.7 us
    pallas_call x1, Pallas kernels, attend_backward(): pl.pallas_call(lambda *refs: attend_grad_kernel(width, depth, *refs), gri...  50 us
    pallas_call x1, Pallas kernels, gather_first(): pl.pallas_call(lambda *refs: gather_kernel(size // PLANE, *refs), out_sha...  29.2 us
    unnamed x3, local copies, waits for them, and re-layouts  7.73 us

profile of v2, /device:TPU:0, one launch (start us, length us, event | category | flops | bytes accessed | tf_op | source)
XLA Modules:
  0.0 213.9 jit_solution(15085127146748389177)
XLA Ops:
  0.6 1.8 copy.22.refs_7_
  2.5 29.2 %gather_first.1 = bf16[16,48,2304]{2,1,0:T(8,128)(2,1)} custom-call(bf16[48,2304]{1,0:T(8,128)(2,1)} %refs_0_.2), custom_call_target="tpu_custom_call" | custom-call | tf_op jit(solution)/shard_map/gather_first/pallas_call | solution.py:224
  31.7 56.7 %attend_forward.1 = (bf16[1024,2304]{1,0:T(8,128)(2,1)}, bf16[1024,768]{1,0:T(8,128)(2,1)}, bf16[16,48,768]{2,1,0:T(8,128)(2,1)}, bf16[16,48,3072]{2,1,0:T(8,128)(2,1)}, bf16[16,192,768]{2,1,0:T(8,128)(2,1)}) custom-call(bf16[1024,768]{1,0:T(8,128)(2,1)} %refs_1_.1, s32[2,1,512]{2,1,0:T(1,128)} %bitcast.9, bf16[768,2304]{1,0:T(8,128)(2,1)} %bitcast.7, ...), custom_call_target="tpu_custom_call" | custom-call | flops 5234491392 | bytes 11403264 | tf_op jit(solution)/shard_map/attend_forward/pallas_call | solution.py:383
  88.5 67.1 %middle.1 = (bf16[1024,768]{1,0:T(8,128)(2,1)}, f32[1024,768]{1,0:T(8,128)}, bf16[1024,768]{1,0:T(8,128)(2,1)}, f32[256,896]{1,0:T(8,128)}) custom-call(bf16[1024,768]{1,0:T(8,128)(2,1)} %get-tuple-element.27.refs_0_, bf16[1024,768]{1,0:T(8,128)(2,1)} %refs_1_.1, bf16[1024,768]{1,0:T(8,128)(2,1)} %refs_2_.1, s32[4,1,256]{2,1,0:T(1,128)} %bitcast.10, ...), custom_call_target="tpu_custom_call" | custom-call | flops 21743271936 | bytes 21626880 | tf_op jit(solution)/shard_map/middle/pallas_call | solution.py:805
  155.6 50.0 %attend_backward.1 = (f32[1024,768]{1,0:T(8,128)}, f32[256,896]{1,0:T(8,128)}) custom-call(bf16[1024,2304]{1,0:T(8,128)(2,1)} %get-tuple-element.32.refs_0_, bf16[1024,768]{1,0:T(8,128)(2,1)} %get-tuple-element.33.refs_1_, s32[2,1,512]{2,1,0:T(1,128)} %bitcast.11, f32[1024,768]{1,0:T(8,128)} %get-tuple-element.34.refs_3_, bf16[768,2304]{1,0:T(8,128)(2,1)} %bitcast.8, ...), custom_call_target="tpu_custom_call" | custom-call | flops 7650410496 | bytes 16121856 | tf_op jit(solution)/shard_map/attend_backward/pallas_call | solution.py:604
  205.6 2.4 %unpack.1 = (f32[1,2]{1,0:T(1,128)}, f32[2,768,64]{2,1,0:T(8,128)}, f32[2,64]{1,0:T(2,128)}, f32[2,64,768]{2,1,0:T(8,128)}, f32[2,768]{1,0:T(2,128)}, /*index=5*/f32[2,768]{1,0:T(2,128)}, f32[2,768]{1,0:T(2,128)}) custom-call(f32[256,896]{1,0:T(8,128)} %get-tuple-element.37.sums_ref), custom_call_target="tpu_custom_call" | custom-call | tf_op jit(solution)/shard_map/unpack/pallas_call | solution.py:643
  208.1 2.1 copy.23
  210.2 3.8 %copy.25 = f32[1024,768]{1,0:T(8,128)} copy(f32[1024,768]{1,0:T(8,128)} %get-tuple-element.64) | data formatting | bytes 6291456

commit v3 on v2

--- a/solution.py
+++ b/solution.py
@@ -9,7 +9,7 @@
 PLANE = 4
 
 
-def gather_stages(depth, z_first, shards, outs, own_sem, send_sem, recv_sem, pair_send, pair_recv):
+def gather_stages(depth, units, shards, outs, own_sem, send_sem, recv_sem, pair_send, pair_recv):
     me = lax.axis_index("dp")
     core = lax.axis_index("head")
     z = me // PLANE
@@ -17,182 +17,144 @@
     step_b = 2 - core
     a = (me // step_a) % 2
     b = (me // step_b) % 2
-    peer_a = z * PLANE + (1 - a) * step_a + b * step_b
-    peer_b = z * PLANE + a * step_a + (1 - b) * step_b
-    up, down = me + PLANE, me - PLANE
     partner = 1 - core
-
-    def has_up():
-        return z < depth - 1
-
-    def has_down():
-        return z > 0
-
-    count = len(outs)
-    pending = []
+    others = [(z + d) % depth for d in range(1, depth)]
+    senders = [(z + depth - d) % depth for d in range(1, depth)]
+    to_a, to_b, to_z = 0, depth, 2 * depth
 
     def owner(z_of, a_of, b_of):
         return z_of * PLANE + a_of * step_a + b_of * step_b
 
-    def guarded(cond, act):
-        if cond is None:
-            act()
-        else:
-            pl.when(cond())(act)
-
-    def send(cond, w, piece, src, dst, direction, slot, target):
-        def copy():
-            return pltpu.make_async_remote_copy(
-                src_ref=src,
-                dst_ref=dst,
-                send_sem=send_sem.at[w, direction, slot],
-                recv_sem=recv_sem.at[w, piece],
-                device_id={"dp": target},
-                device_id_type=MESH,
-            )
-
-        guarded(cond, lambda: copy().start())
-        pending.append((cond, w, send_sem, (w, direction, slot)))
-
-    def hand(cond, w, piece, view):
-        def copy():
-            return pltpu.make_async_remote_copy(
-                src_ref=view,
-                dst_ref=view,
-                send_sem=pair_send.at[w, piece],
-                recv_sem=pair_recv.at[w, piece],
-                device_id={"head": partner},
-                device_id_type=MESH,
-            )
-
-        guarded(cond, lambda: copy().start())
-
-    def view_of(w, piece, side):
+    peer_a = owner(z, 1 - a, b)
+    peer_b = owner(z, a, 1 - b)
+
+    def view_of(u, piece, side):
+        w, row, height, col, span, _ = units[u]
         half = outs[w].shape[2] // 2
-        return outs[w].at[piece, :, pl.ds(pl.multiple_of(side * half, 128), half)]
+        at = pl.ds(pl.multiple_of(side * half + col, 128), span)
+        return outs[w].at[piece, row : row + height, at]
+
+    def shard_of(u):
+        w, row, height, col, span, _ = units[u]
+        half = outs[w].shape[2] // 2
+        at = pl.ds(pl.multiple_of(core * half + col, 128), span)
+        return shards[w].at[row : row + height, at]
 
     def wait(sem, view):
         pltpu.make_async_copy(view, view, sem).wait()
 
-    def arrive(cond, w, piece):
-        view = view_of(w, piece, core)
-        guarded(cond, lambda: wait(recv_sem.at[w, piece], view))
+    def send(u, piece, src, slot, target):
+        pltpu.make_async_remote_copy(
+            src_ref=src,
+            dst_ref=view_of(u, piece, core),
+            send_sem=send_sem.at[u, slot],
+            recv_sem=recv_sem.at[u, piece],
+            device_id={"dp": target},
+            device_id_type=MESH,
+        ).start()
+
+    def hand(u, piece):
+        view = view_of(u, piece, core)
+        pltpu.make_async_remote_copy(
+            src_ref=view,
+            dst_ref=view,
+            send_sem=pair_send.at[u, piece],
+            recv_sem=pair_recv.at[u, piece],
+            device_id={"head": partner},
+            device_id_type=MESH,
+        ).start()
+
+    def arrive(u, piece):
+        view = view_of(u, piece, core)
+        wait(recv_sem.at[u, piece], view)
         return view
+
+    def z_slot(k, d):
+        return to_z + k * (depth - 1) + d
+
+    def b_slot(k):
+        return to_z + 2 * (depth - 1) + k
 
     def start():
         barrier = pltpu.get_barrier_semaphore()
-
-        def greet(cond, target):
-            guarded(
-                cond,
-                lambda: pl.semaphore_signal(
-                    barrier, inc=1, device_id=target, device_id_type=MESH
-                ),
-            )
-
-        greet(None, {"dp": peer_a})
-        greet(None, {"dp": peer_b})
-        greet(None, {"head": partner})
-        greet(has_up, {"dp": up})
-        greet(has_down, {"dp": down})
-        pl.semaphore_wait(barrier, 3 + has_up().astype(jnp.int32) + has_down().astype(jnp.int32))
-        for w in range(count):
-            half = outs[w].shape[2] // 2
-            src = shards[w].at[:, pl.ds(pl.multiple_of(core * half, 128), half)]
-            view = view_of(w, me, core)
-            send(None, w, me, src, view, 0, 0, peer_a)
-            send(has_up, w, me, src, view, 1, 0, up)
-            send(has_down, w, me, src, view, 2, 0, down)
-            send(None, w, me, src, view, 3, 0, peer_b)
-        for w in range(count):
+        targets = [{"head": partner}, {"dp": peer_a}, {"dp": peer_b}]
+        targets += [{"dp": owner(z_of, a, b)} for z_of in others]
+        for target in targets:
+            pl.semaphore_signal(barrier, inc=1, device_id=target, device_id_type=MESH)
+        pl.semaphore_wait(barrier, depth + 2)
+        for u in range(len(units)):
+            src = shard_of(u)
+            send(u, me, src, to_a, peer_a)
+            for d, z_of in enumerate(others):
+                send(u, me, src, z_slot(0, d), owner(z_of, a, b))
+            send(u, me, src, to_b, peer_b)
+        for w in range(len(outs)):
             pltpu.make_async_copy(shards[w], outs[w].at[me], own_sem.at[w]).start()
 
-    def first(w):
-        if z_first[w]:
-            return
-        view = arrive(None, w, peer_a)
-        send(has_up, w, peer_a, view, view, 1, 1, up)
-        send(has_down, w, peer_a, view, view, 2, 1, down)
-        send(None, w, peer_a, view, view, 3, 1, peer_b)
-        hand(None, w, peer_a, view)
-
-    def line(w, dist):
-        for k, a_of in enumerate((a,) if z_first[w] else (a, 1 - a)):
-            slot = 2 * dist + k
-            for above in (False, True):
-                z_of = z + dist if above else z - dist
-
-                def there(above=above):
-                    return z + dist < depth if above else z >= dist
-
-                def onward(above=above):
-                    inner = z > 0 if above else z < depth - 1
-                    return jnp.logical_and(there(above), inner)
-
+    def first(u):
+        view = arrive(u, peer_a)
+        for d, z_of in enumerate(others):
+            send(u, peer_a, view, z_slot(1, d), owner(z_of, a, b))
+        send(u, peer_a, view, to_b + 1, peer_b)
+        hand(u, peer_a)
+
+    def line(u):
+        along = units[u][5]
+        for d, z_of in enumerate(senders):
+            for k, a_of in enumerate((a,) if along else (a, 1 - a)):
                 piece = owner(z_of, a_of, b)
-                view = arrive(there, w, piece)
-                if above:
-                    send(onward, w, piece, view, view, 2, slot, down)
-                else:
-                    send(onward, w, piece, view, view, 1, slot, up)
-                late = 2 * depth * above + slot
-                if z_first[w]:
-                    send(there, w, piece, view, view, 0, late, peer_a)
-                send(there, w, piece, view, view, 3, late, peer_b)
-                hand(there, w, piece, view)
-
-    def across(w):
-        for z_of in range(depth):
+                view = arrive(u, piece)
+                if along:
+                    send(u, piece, view, to_a + 1 + d, peer_a)
+                send(u, piece, view, b_slot(2 * d + k), peer_b)
+                hand(u, piece)
+
+    def across(u):
+        for n, z_of in enumerate([z] + senders):
             piece = owner(z_of, 1 - a, b)
-            view = arrive(None, w, piece)
-            send(None, w, piece, view, view, 3, 4 * depth + z_of, peer_b)
-            hand(None, w, piece, view)
-
-    def last(w):
-        for z_of in range(depth):
-            for a_of in range(2):
+            view = arrive(u, piece)
+            send(u, piece, view, b_slot(2 * n - 1) if n else to_b + 1, peer_b)
+            hand(u, piece)
+
+    def last(u):
+        for z_of in [z] + senders:
+            for a_of in (a, 1 - a):
                 piece = owner(z_of, a_of, 1 - b)
-                hand(None, w, piece, arrive(None, w, piece))
+                arrive(u, piece)
+                hand(u, piece)
 
     def finish():
-        for w in range(count):
+        for w in range(len(outs)):
             wait(own_sem.at[w], outs[w].at[me])
+        for u, unit in enumerate(units):
             for z_of in range(depth):
                 for a_of in range(2):
                     for b_of in range(2):
                         piece = owner(z_of, a_of, b_of)
 
-                        def pair(w=w, piece=piece):
-                            wait(pair_recv.at[w, piece], view_of(w, piece, partner))
-                            wait(pair_send.at[w, piece], view_of(w, piece, core))
+                        def pair(u=u, piece=piece):
+                            wait(pair_recv.at[u, piece], view_of(u, piece, partner))
+                            wait(pair_send.at[u, piece], view_of(u, piece, core))
 
                         pl.when(piece != me)(pair)
-        for cond, w, sem, at in pending:
-            guarded(cond, lambda: wait(sem.at[at], view_of(w, me, core)))
-
-    def firsts():
-        for w in range(count):
-            first(w)
-
-    stages = [start, firsts]
-    for dist in range(1, depth):
-        for w in range(count):
-            stages.append(lambda w=w, dist=dist: line(w, dist))
-    for w in range(count):
-        if z_first[w]:
-            stages.append(lambda w=w: across(w))
-    for w in range(count):
-        stages.append(lambda w=w: last(w))
-    return stages + [finish]
-
-
-def gather_scratch(count, size):
+            slots = [to_a, to_b, to_b + 1]
+            slots += [z_slot(k, d) for k in range(1 if unit[5] else 2) for d in range(depth - 1)]
+            slots += [b_slot(n) for n in range(2 * (depth - 1))]
+            if unit[5]:
+                slots += [to_a + 1 + d for d in range(depth - 1)]
+            for slot in slots:
+                wait(send_sem.at[u, slot], view_of(u, me, core))
+
+    return start, first, line, across, last, finish
+
+
+def gather_scratch(count, units, size):
     return [
         pltpu.SemaphoreType.DMA((count,)),
-        pltpu.SemaphoreType.DMA((count, 4, 5 * (size // PLANE))),
-        pltpu.SemaphoreType.DMA((count, size)),
-        pltpu.SemaphoreType.DMA((count, size)),
-        pltpu.SemaphoreType.DMA((count, size)),
+        pltpu.SemaphoreType.DMA((units, 6 * (size // PLANE))),
+        pltpu.SemaphoreType.DMA((units, size)),
+        pltpu.SemaphoreType.DMA((units, size)),
+        pltpu.SemaphoreType.DMA((units, size)),
     ]
 
 
@@ -201,7 +163,8 @@
     return (
         size % PLANE == 0
         and size > PLANE
-        and all(w.shape[0] % 16 == 0 and w.shape[1] % 256 == 0 for w in weights)
+        and all(w.shape[0] % 16 == 0 and w.shape[1] % 768 == 0 for w in weights)
+        and weights[-1].shape[0] % 32 in (0, 16 * (len(weights) == 1))
     )
 
 
@@ -214,23 +177,81 @@
     return pieces.reshape(-1, pieces.shape[-1])
 
 
-def gather_kernel(depth, *refs):
-    for stage in gather_stages(depth, (False,), refs[:1], refs[1:2], *refs[2:]):
-        stage()
+def first_units(weight):
+    rows, width = weight.shape
+    third = width // 6
+    return [(0, 0, rows, n * third, third, n > 0) for n in range(3)]
+
+
+def gather_kernel(depth, units, *refs):
+    start, first, line, across, last, finish = gather_stages(
+        depth, units, refs[:1], refs[1:2], *refs[2:]
+    )
+    start()
+    first(0)
+    for u in (1, 2, 0):
+        line(u)
+    for u in (1, 2):
+        across(u)
+    for u in (0, 1, 2):
+        last(u)
+    finish()
 
 
 def gather_first(weight):
     size = lax.axis_size("dp")
+    units = first_units(weight)
     gathered = pl.pallas_call(
-        lambda *refs: gather_kernel(size // PLANE, *refs),
+        lambda *refs: gather_kernel(size // PLANE, units, *refs),
         out_shape=gather_shapes([weight]),
         in_specs=[pl.BlockSpec(memory_space=pltpu.VMEM)],
         out_specs=[pl.BlockSpec(memory_space=pl.ANY)],
-        scratch_shapes=gather_scratch(1, size),
+        scratch_shapes=gather_scratch(1, len(units), size),
         compiler_params=pltpu.CompilerParams(collective_id=0, has_side_effects=True),
         name="gather_first",
     )(weight)
     return join(gathered[0])
+
+
+def later_units(weights):
+    out, expand, reduce = (w.shape for w in weights)
+    quarter = expand[1] // 4
+    rows = reduce[0] // 2
+    return [
+        (0, 0, out[0], 0, out[1] // 2, False),
+        (1, 0, expand[0], 0, quarter, False),
+        (1, 0, expand[0], quarter, quarter, True),
+        (2, 0, rows, 0, reduce[1] // 2, True),
+        (2, rows, rows, 0, reduce[1] // 2, True),
+    ]
+
+
+def later_stages(start, first, line, across, last, finish):
+    def both(one, two):
+        def run():
+            one()
+            two()
+
+        return run
+
+    def of(act, u):
+        return lambda: act(u)
+
+    return [
+        both(of(first, 0), of(first, 1)),
+        of(line, 2),
+        of(line, 3),
+        of(line, 4),
+        of(line, 0),
+        of(across, 2),
+        of(line, 1),
+        of(across, 3),
+        of(across, 4),
+        both(of(last, 0), of(last, 2)),
+        of(last, 1),
+        of(last, 3),
+        of(last, 4),
+    ]
 
 
 HEAD_DIM = 64
@@ -300,11 +321,13 @@
     return pl.ds(pl.multiple_of(start, 128), width)
 
 
-def attend_kernel(width, depth, *refs):
+def attend_kernel(width, depth, units, *refs):
     hid_ref, seg_ref, w_ref = refs[:3]
     if depth:
         shards, (qkv_ref, ctx_ref), outs, bias_ref = refs[3:6], refs[6:8], refs[8:11], refs[11]
-        start, *stages, finish = gather_stages(depth, Z_FIRST, shards, outs, *refs[12:])
+        moves = gather_stages(depth, units, shards, outs, *refs[12:])
+        stages = later_stages(*moves)
+        start, finish = moves[0], moves[-1]
         pl.when(pl.program_id(0) == 0)(start)
     else:
         qkv_ref, ctx_ref, bias_ref = refs[3:]
@@ -348,7 +371,6 @@
             finish()
 
 
-Z_FIRST = (False, False, True)
 SLOTS = 12
 
 
@@ -357,6 +379,7 @@
     size = lax.axis_size("dp")
     fits = gather_fits(shards) and rows // SEQ_LEN * (width // PAIR) >= SLOTS
     depth = size // PLANE if fits else 0
+    units = later_units(shards)
     operands = [hidden, seg_rows, weight_in]
     in_specs = [
         pl.BlockSpec((SEQ_LEN, width), lambda i: (i, 0)),
@@ -378,10 +401,10 @@
         in_specs += [pl.BlockSpec(w.shape, lambda i: (0, 0)) for w in shards]
         out_shape += gather_shapes(shards)
         out_specs += [pl.BlockSpec(memory_space=pl.ANY)] * len(shards)
-        scratch += gather_scratch(len(shards), size)
+        scratch += gather_scratch(len(shards), len(units), size)
         settings |= {"collective_id": 2, "has_side_effects": True}
     qkv, ctx, *gathered = pl.pallas_call(
-        lambda *refs: attend_kernel(width, depth, *refs),
+        lambda *refs: attend_kernel(width, depth, units, *refs),
         grid=(rows // SEQ_LEN,),
         out_shape=out_shape,
         in_specs=in_specs,
@@ -621,9 +644,8 @@
 
 def unpack_kernel(sums_ref, ratio_ref, down_ref, down_bias_ref, up_ref, up_bias_ref, gain_ref, shift_ref):
     rank, width = up_ref.shape[1:]
-    tall = sums_ref[: 2 * rank, :width].T
     for k in range(2):
-        down_ref[k] = tall[:, k * rank : (k + 1) * rank]
+        down_ref[k] = sums_ref[k * rank : (k + 1) * rank, :width]
         up_ref[k] = sums_ref[(2 + k) * rank : (3 + k) * rank, :width]
     for n in range(width // 128):
         at = slice(128 * n, 128 * n + 128)
@@ -639,13 +661,13 @@
 
 def unpack(sums, rank):
     width = sums.shape[1] - 128
-    shapes = [(1, 2), (2, width, rank), (2, rank), (2, rank, width)] + [(2, width)] * 3
-    ratio, *rest = pl.pallas_call(
+    shapes = [(1, 2), (2, rank, width), (2, rank), (2, rank, width)] + [(2, width)] * 3
+    ratio, down, *rest = pl.pallas_call(
         unpack_kernel,
         out_shape=[jax.ShapeDtypeStruct(shape, jnp.float32) for shape in shapes],
         name="unpack",
     )(sums)
-    return (ratio.reshape(2), *rest)
+    return (ratio.reshape(2), jnp.transpose(down, (0, 2, 1)), *rest)
 
 
 def row_mean(x):
@@ -703,7 +725,7 @@
 
     def adapter(k, a):
         a_low = a.astype(jnp.bfloat16)
-        act, slope = gelu_pair(dot(a_low, down_ref[k]) + down_bias_ref[k : k + 1, :])
+        act, slope = gelu_pair(dot_nt(a_low, down_ref[k]) + down_bias_ref[k : k + 1, :])
         act = act.astype(jnp.bfloat16)
         branch = dot(act, up_ref[k]) + up_bias_ref[k : k + 1, :]
         ratio = jnp.sqrt(row_mean(branch * branch)) / jnp.sqrt(row_mean(a * a) + EPS_RATIO)
@@ -721,7 +743,7 @@
         sums_ref[(2 + k) * rank : (3 + k) * rank, :width] += dot_tn(act, grad_low)
         add(k, col_sum(grad_low.astype(jnp.float32)))
         add(6 + k, col_sum(hidden_grad.astype(jnp.float32)))
-        return (grad + dot_nt(hidden_grad, down_ref[k])).astype(jnp.bfloat16)
+        return (grad + dot(hidden_grad, down_ref[k])).astype(jnp.bfloat16)
 
     gain_one, gain_two = gain_ref[0:1, :], gain_ref[1:2, :]
     attended = dot(ctx_ref[...], wo_ref[...])
@@ -784,7 +806,7 @@
             sums_ref[8 * n : 8 * n + 8, width:] = small_ref[:, 128 * n : 128 * n + 128]
 
 
-TILE = 256
+TILE = 512
 CHUNK = 512
 SUM_ROWS = 256
 
@@ -854,7 +876,7 @@
     shards = [output_weight, expand_weight, reduce_weight]
     qkv, ctx, frozen = attend_forward(hidden_states, seg_rows, weight_in, shards)
     params = (
-        adapter_down,
+        jnp.transpose(adapter_down, (0, 2, 1)),
         adapter_down_bias,
         adapter_up,
         adapter_up_bias,

time: 214 us -> 214 us (level)
  local copies, waits for them, and re-layouts: 7.73 us -> 3.76 us
  Pallas kernels: 206 us -> 209 us
    pallas_call x2, Pallas kernels: 86 us -> 99.9 us  [the longest x1 68.6 us: attend_forward(): pl.pallas_call(lambda *refs: attend_kernel(width, depth, units, *refs), g...]
    pallas_call x1, Pallas kernels: 67.1 us -> 60.4 us  [middle(): pl.pallas_call(lambda *refs: middle_kernel(ff, CHUNK, *refs), grid=(rows...]
    unnamed x3 -> x1, local copies, waits for them, and re-layouts: 7.73 us -> 3.76 us
    pallas_call x1, Pallas kernels: 50 us -> 46.8 us  [attend_backward(): pl.pallas_call(lambda *refs: attend_grad_kernel(width, depth, *refs), gri...]
where the time goes in v3:
time: 214 us
  Pallas kernels  209 us (98%)
  local copies, waits for them, and re-layouts  3.76 us (2%)
    pallas_call x1, Pallas kernels, attend_forward(): pl.pallas_call(lambda *refs: attend_kernel(width, depth, units, *refs), g...  68.6 us
    pallas_call x1, Pallas kernels, middle(): pl.pallas_call(lambda *refs: middle_kernel(ff, CHUNK, *refs), grid=(rows...  60.4 us
    pallas_call x1, Pallas kernels, attend_backward(): pl.pallas_call(lambda *refs: attend_grad_kernel(width, depth, *refs), gri...  46.8 us
    pallas_call x1, Pallas kernels, gather_first(): pl.pallas_call(lambda *refs: gather_kernel(size // PLANE, units, *refs),...  31.3 us

profile of v3, /device:TPU:0, one launch (start us, length us, event | category | flops | bytes accessed | tf_op | source)
XLA Modules:
  0.0 213.6 jit_solution(13124641420285621865)
XLA Ops:
  0.6 31.3 %gather_first.1 = bf16[16,48,2304]{2,1,0:T(8,128)(2,1)} custom-call(bf16[48,2304]{1,0:T(8,128)(2,1)} %refs_0_.2), custom_call_target="tpu_custom_call" | custom-call | tf_op jit(solution)/shard_map/gather_first/pallas_call | solution.py:204
  32.0 68.6 %attend_forward.1 = (bf16[1024,2304]{1,0:T(8,128)(2,1)}, bf16[1024,768]{1,0:T(8,128)(2,1)}, bf16[16,48,768]{2,1,0:T(8,128)(2,1)}, bf16[16,48,3072]{2,1,0:T(8,128)(2,1)}, bf16[16,192,768]{2,1,0:T(8,128)(2,1)}) custom-call(bf16[1024,768]{1,0:T(8,128)(2,1)} %refs_1_.1, s32[2,1,512]{2,1,0:T(1,128)} %bitcast.12, bf16[768,2304]{1,0:T(8,128)(2,1)} %bitcast.8, ...), custom_call_target="tpu_custom_call" | custom-call | flops 5234491392 | bytes 11403264 | tf_op jit(solution)/shard_map/attend_forward/pallas_call | solution.py:406
  100.6 60.4 %middle.1 = (bf16[1024,768]{1,0:T(8,128)(2,1)}, f32[1024,768]{1,0:T(8,128)}, bf16[1024,768]{1,0:T(8,128)(2,1)}, f32[256,896]{1,0:T(8,128)}) custom-call(bf16[1024,768]{1,0:T(8,128)(2,1)} %get-tuple-element.27.refs_0_, bf16[1024,768]{1,0:T(8,128)(2,1)} %refs_1_.1, bf16[1024,768]{1,0:T(8,128)(2,1)} %refs_2_.1, s32[2,1,512]{2,1,0:T(1,128)} %bitcast.13, ...), custom_call_target="tpu_custom_call" | custom-call | flops 21743271936 | bytes 21626880 | tf_op jit(solution)/shard_map/middle/pallas_call | solution.py:827
  160.9 46.8 %attend_backward.1 = (f32[1024,768]{1,0:T(8,128)}, f32[256,896]{1,0:T(8,128)}) custom-call(bf16[1024,2304]{1,0:T(8,128)(2,1)} %get-tuple-element.32.refs_0_, bf16[1024,768]{1,0:T(8,128)(2,1)} %get-tuple-element.33.refs_1_, s32[2,1,512]{2,1,0:T(1,128)} %bitcast.14, f32[1024,768]{1,0:T(8,128)} %get-tuple-element.34.refs_3_, bf16[768,2304]{1,0:T(8,128)(2,1)} %bitcast.9, ...), custom_call_target="tpu_custom_call" | custom-call | flops 7650410496 | bytes 16121856 | tf_op jit(solution)/shard_map/attend_backward/pallas_call | solution.py:627
  207.8 2.1 unpack.1
  209.9 3.8 %copy.23 = f32[1024,768]{1,0:T(8,128)} copy(f32[1024,768]{1,0:T(8,128)} %get-tuple-element.55) | data formatting | bytes 6291456

commit v4 on v2

--- a/solution.py
+++ b/solution.py
@@ -621,9 +621,8 @@
 
 def unpack_kernel(sums_ref, ratio_ref, down_ref, down_bias_ref, up_ref, up_bias_ref, gain_ref, shift_ref):
     rank, width = up_ref.shape[1:]
-    tall = sums_ref[: 2 * rank, :width].T
     for k in range(2):
-        down_ref[k] = tall[:, k * rank : (k + 1) * rank]
+        down_ref[k] = sums_ref[k * rank : (k + 1) * rank, :width]
         up_ref[k] = sums_ref[(2 + k) * rank : (3 + k) * rank, :width]
     for n in range(width // 128):
         at = slice(128 * n, 128 * n + 128)
@@ -639,13 +638,13 @@
 
 def unpack(sums, rank):
     width = sums.shape[1] - 128
-    shapes = [(1, 2), (2, width, rank), (2, rank), (2, rank, width)] + [(2, width)] * 3
-    ratio, *rest = pl.pallas_call(
+    shapes = [(1, 2), (2, rank, width), (2, rank), (2, rank, width)] + [(2, width)] * 3
+    ratio, down, *rest = pl.pallas_call(
         unpack_kernel,
         out_shape=[jax.ShapeDtypeStruct(shape, jnp.float32) for shape in shapes],
         name="unpack",
     )(sums)
-    return (ratio.reshape(2), *rest)
+    return (ratio.reshape(2), jnp.transpose(down, (0, 2, 1)), *rest)
 
 
 def row_mean(x):
@@ -703,7 +702,7 @@
 
     def adapter(k, a):
         a_low = a.astype(jnp.bfloat16)
-        act, slope = gelu_pair(dot(a_low, down_ref[k]) + down_bias_ref[k : k + 1, :])
+        act, slope = gelu_pair(dot_nt(a_low, down_ref[k]) + down_bias_ref[k : k + 1, :])
         act = act.astype(jnp.bfloat16)
         branch = dot(act, up_ref[k]) + up_bias_ref[k : k + 1, :]
         ratio = jnp.sqrt(row_mean(branch * branch)) / jnp.sqrt(row_mean(a * a) + EPS_RATIO)
@@ -721,7 +720,7 @@
         sums_ref[(2 + k) * rank : (3 + k) * rank, :width] += dot_tn(act, grad_low)
         add(k, col_sum(grad_low.astype(jnp.float32)))
         add(6 + k, col_sum(hidden_grad.astype(jnp.float32)))
-        return (grad + dot_nt(hidden_grad, down_ref[k])).astype(jnp.bfloat16)
+        return (grad + dot(hidden_grad, down_ref[k])).astype(jnp.bfloat16)
 
     gain_one, gain_two = gain_ref[0:1, :], gain_ref[1:2, :]
     attended = dot(ctx_ref[...], wo_ref[...])
@@ -784,7 +783,7 @@
             sums_ref[8 * n : 8 * n + 8, width:] = small_ref[:, 128 * n : 128 * n + 128]
 
 
-TILE = 256
+TILE = 512
 CHUNK = 512
 SUM_ROWS = 256
 
@@ -854,7 +853,7 @@
     shards = [output_weight, expand_weight, reduce_weight]
     qkv, ctx, frozen = attend_forward(hidden_states, seg_rows, weight_in, shards)
     params = (
-        adapter_down,
+        jnp.transpose(adapter_down, (0, 2, 1)),
         adapter_down_bias,
         adapter_up,
         adapter_up_bias,

time: 214 us -> 203 us (0.949)
  Pallas kernels: 206 us -> 198 us
  local copies, waits for them, and re-layouts: 7.73 us -> 3.76 us
    pallas_call x1, Pallas kernels: 67.1 us -> 60.4 us  [middle(): pl.pallas_call(lambda *refs: middle_kernel(ff, CHUNK, *refs), grid=(rows...]
    unnamed x3 -> x1, local copies, waits for them, and re-layouts: 7.73 us -> 3.76 us
where the time goes in v4:
time: 203 us
  Pallas kernels  198 us (98%)
  local copies, waits for them, and re-layouts  3.76 us (2%)
    pallas_call x1, Pallas kernels, middle(): pl.pallas_call(lambda *refs: middle_kernel(ff, CHUNK, *refs), grid=(rows...  60.4 us
    pallas_call x1, Pallas kernels, attend_forward(): pl.pallas_call(lambda *refs: attend_kernel(width, depth, *refs), grid=(ro...  56.7 us
    pallas_call x1, Pallas kernels, attend_backward(): pl.pallas_call(lambda *refs: attend_grad_kernel(width, depth, *refs), gri...  49.9 us
    pallas_call x1, Pallas kernels, gather_first(): pl.pallas_call(lambda *refs: gather_kernel(size // PLANE, *refs), out_sha...  29.2 us

profile of v4, /device:TPU:0, one launch (start us, length us, event | category | flops | bytes accessed | tf_op | source)
XLA Modules:
  0.0 202.7 jit_solution(4103473949571599099)
XLA Ops:
  0.6 29.2 %gather_first.1 = bf16[16,48,2304]{2,1,0:T(8,128)(2,1)} custom-call(bf16[48,2304]{1,0:T(8,128)(2,1)} %refs_0_.2), custom_call_target="tpu_custom_call" | custom-call | tf_op jit(solution)/shard_map/gather_first/pallas_call | solution.py:224
  29.9 56.7 %attend_forward.1 = (bf16[1024,2304]{1,0:T(8,128)(2,1)}, bf16[1024,768]{1,0:T(8,128)(2,1)}, bf16[16,48,768]{2,1,0:T(8,128)(2,1)}, bf16[16,48,3072]{2,1,0:T(8,128)(2,1)}, bf16[16,192,768]{2,1,0:T(8,128)(2,1)}) custom-call(bf16[1024,768]{1,0:T(8,128)(2,1)} %refs_1_.1, s32[2,1,512]{2,1,0:T(1,128)} %bitcast.12, bf16[768,2304]{1,0:T(8,128)(2,1)} %bitcast.8, ...), custom_call_target="tpu_custom_call" | custom-call | flops 5234491392 | bytes 11403264 | tf_op jit(solution)/shard_map/attend_forward/pallas_call | solution.py:383
  86.6 60.4 %middle.1 = (bf16[1024,768]{1,0:T(8,128)(2,1)}, f32[1024,768]{1,0:T(8,128)}, bf16[1024,768]{1,0:T(8,128)(2,1)}, f32[256,896]{1,0:T(8,128)}) custom-call(bf16[1024,768]{1,0:T(8,128)(2,1)} %get-tuple-element.27.refs_0_, bf16[1024,768]{1,0:T(8,128)(2,1)} %refs_1_.1, bf16[1024,768]{1,0:T(8,128)(2,1)} %refs_2_.1, s32[2,1,512]{2,1,0:T(1,128)} %bitcast.13, ...), custom_call_target="tpu_custom_call" | custom-call | flops 21743271936 | bytes 21626880 | tf_op jit(solution)/shard_map/middle/pallas_call | solution.py:804
  147.0 49.9 %attend_backward.1 = (f32[1024,768]{1,0:T(8,128)}, f32[256,896]{1,0:T(8,128)}) custom-call(bf16[1024,2304]{1,0:T(8,128)(2,1)} %get-tuple-element.32.refs_0_, bf16[1024,768]{1,0:T(8,128)(2,1)} %get-tuple-element.33.refs_1_, s32[2,1,512]{2,1,0:T(1,128)} %bitcast.14, f32[1024,768]{1,0:T(8,128)} %get-tuple-element.34.refs_3_, bf16[768,2304]{1,0:T(8,128)(2,1)} %bitcast.9, ...), custom_call_target="tpu_custom_call" | custom-call | flops 7650410496 | bytes 16121856 | tf_op jit(solution)/shard_map/attend_backward/pallas_call | solution.py:604
  196.9 2.1 %unpack.1 = (f32[1,2]{1,0:T(1,128)}, f32[2,64,768]{2,1,0:T(8,128)}, f32[2,64]{1,0:T(2,128)}, f32[2,64,768]{2,1,0:T(8,128)}, f32[2,768]{1,0:T(2,128)}, /*index=5*/f32[2,768]{1,0:T(2,128)}, f32[2,768]{1,0:T(2,128)}) custom-call(f32[256,896]{1,0:T(8,128)} %get-tuple-element.37.sums_ref), custom_call_target="tpu_custom_call" | custom-call | tf_op jit(solution)/shard_map/unpack/pallas_call | solution.py:642
  198.9 3.8 %copy.23 = f32[1024,768]{1,0:T(8,128)} copy(f32[1024,768]{1,0:T(8,128)} %get-tuple-element.55) | data formatting | bytes 6291456
